TPU v7x, 32 devices: a whole 2x2x4 slice. The times are simulated.
32 devices in a mesh: dp: 4 (over y, x), vocab: 8 (over z, core).
Axes of the slice: x: 2, y: 2, z: 4, core: 2. Of those that a mesh axis runs over, the one named last changes fastest.
Arguments:
- prefill_hidden: bfloat16 [128, 7168], P(('dp', 'vocab')), may hold values from -60 to 60
- decode_hidden: bfloat16 [32, 7168], P(('dp', 'vocab')), may hold values from -60 to 60
- lm_head: bfloat16 [7168, 16160], P('dp', 'vocab'), as said below
- prefill_targets: int32 [128], P(('dp', 'vocab')), may hold values from 0 to 16159
- decode_targets: int32 [32], P(('dp', 'vocab')), may hold values from 0 to 16159
- decode_live: int32 [4], P('dp'), may hold values from 1 to 8
Outputs:
- prefill_logprob: float32 [128], P(('dp', 'vocab'))
- decode_logprob: float32 [32], P(('dp', 'vocab'))
Inputs may be any that keep to these rules, and one draw needn't show every extreme that they name: `lm_head`: entries of order one over the square root of 7168.
All inputs are finite; a program needn't handle non-finite values.
Results may differ from a plain program's by a relative error of at most 0.0003.
Values may be sent and summed in bfloat16 or wider, within the bound.
No kernel may reach another device: no remote copies, remote signals or barrier semaphores. Data moves between devices by JAX's collectives and lax.ppermute only.
A program may use at most 128 MiB of HBM per device.

v0:
```python
import jax
import jax.numpy as jnp
from jax import lax
from jax.sharding import PartitionSpec as P


def body(prefill_hidden, decode_hidden, lm_head, prefill_targets, decode_targets, decode_live):
    pre_rows = prefill_hidden.shape[0]
    dec_rows = decode_hidden.shape[0]
    own_count = pre_rows + dec_rows
    hidden = jnp.concatenate([prefill_hidden, decode_hidden], axis=0)
    targets = jnp.concatenate([prefill_targets, decode_targets], axis=0)
    shard_vocab = lm_head.shape[1]
    vocab_offset = lax.axis_index("vocab") * shard_vocab
    group_hidden, group_targets = (
        lax.all_gather(hidden, "vocab", axis=0, tiled=True),
        lax.all_gather(targets, "vocab", axis=0, tiled=True),
    )
    every_rows = lax.all_to_all(group_hidden, "dp", split_axis=1, concat_axis=0, tiled=True)
    logits = lax.psum_scatter(
        jnp.dot(every_rows, lm_head, preferred_element_type=jnp.float32),
        "dp",
        scatter_dimension=0,
        tiled=True,
    )
    local_top = jnp.max(logits, axis=1)
    target_hit = (group_targets - vocab_offset)[:, None] == jnp.arange(
        shard_vocab, dtype=jnp.int32
    )[None, :]
    local_picked = jnp.sum(jnp.where(target_hit, logits, jnp.float32(0.0)), axis=1)
    own_start = lax.axis_index("vocab") * own_count
    row_top = lax.pmax(local_top, "vocab")
    local_total = jnp.sum(jnp.exp(logits - row_top[:, None]), axis=1)
    totals, picked = lax.psum((local_total, local_picked), "vocab")
    group_values = picked - (row_top + jnp.log(totals))
    own_values = lax.dynamic_slice_in_dim(group_values, own_start, own_count, 0)
    prefill_logprob = own_values[:pre_rows]
    positions = lax.axis_index("vocab") * dec_rows + jnp.arange(dec_rows, dtype=jnp.int32)
    decode_logprob = jnp.where(positions < decode_live[0], own_values[pre_rows:], jnp.float32(0.0))
    return (prefill_logprob, decode_logprob)


def solution(mesh):
    in_specs = (
        P(("dp", "vocab"), None),
        P(("dp", "vocab"), None),
        P("dp", "vocab"),
        P(("dp", "vocab")),
        P(("dp", "vocab")),
        P("dp"),
    )
    out_specs = (P(("dp", "vocab")), P(("dp", "vocab")))
    return jax.shard_map(body, mesh=mesh, in_specs=in_specs, out_specs=out_specs, check_vma=False)
```

profile of v0, /device:TPU:0, one launch (start us, length us, event | category | flops | bytes accessed | tf_op | source)
XLA Modules:
  0.0 116.8 jit_solution(9605477121239586276)
XLA Ops:
  7.2 0.0 reduce-scatter.4.cloned.1.call-start
  7.2 0.9 maximum_bitcast_fusion
  8.1 17.6 %all-gather = bf16[8,5,7168]{2,1,0:T(8,128)(2,1)S(1)} all-gather(bf16[1,5,7168]{2,1,0:T(8,128)(2,1)S(1)} %maximum_bitcast_fusion), channel_id=1, replica_groups=mesh['dp'=4,'vocab'=8] {'vocab'}, dimensions={0}, use_global_device_ids=true | all-gather | bytes 645120 | tf_op jit(solution)/shard_map/all_gather | solution.py:16
  25.7 0.0 copy-start.1
  25.7 0.0 copy-start
  25.7 0.5 all_to_all.14
  26.2 0.1 copy.9
  26.3 13.3 %all_to_all.19 = bf16[40,4,1792]{2,0,1:T(8,128)(2,1)S(1)} all-to-all(bf16[40,4,1792]{2,0,1:T(8,128)(2,1)S(1)} %copy.9), channel_id=1, replica_groups=mesh['dp'=4,'vocab'=8] {'dp'}, dimensions={1} | all-to-all | bytes 1146880 | tf_op jit(solution)/shard_map/all_to_all | solution.py:19
  39.6 6.6 %fusion = f32[160,2020]{1,0:T(8,128)} fusion(bf16[160,1792]{1,0:T(8,128)(2,1)S(1)} %bitcast.11, bf16[1792,2020]{0,1:T(8,128)(2,1)} %param.8), kind=kOutput, calls=%fused_computation.7 | convolution fusion | flops 1158348800 | bytes 9105920 | tf_op jit(solution)/shard_map/dot_general | solution.py:21
  46.1 0.0 reduce-scatter.4.cloned.1.call-update
  47.5 0.0 copy-done.1
  47.5 0.6 dynamic-slice
  48.7 0.0 copy-done
  48.7 0.2 add_dynamic-update-slice_fusion
  48.9 9.3 %all-reduce = s32[40]{0:T(128)S(1)} all-reduce(s32[40]{0:T(128)S(1)} %add_dynamic-update-slice_fusion), channel_id=1, replica_groups=mesh['dp'=4,'vocab'=8] {'vocab'}, use_global_device_ids=true, to_apply=%add | all-reduce | flops 40 | bytes 320
  58.2 17.2 %reduce-scatter.4.cloned.1.call-done = f32[40,2020]{1,0:T(8,128)} async-done(((f32[160,2020]{1,0:T(8,128)}), f32[40,2020]{1,0:T(8,128)}) %reduce-scatter.4.cloned.1.call-update) | async-done | bytes 323216
  75.4 1.1 reduce_max.9
  76.5 16.2 %pmax.7 = f32[40]{0:T(128)S(1)} all-reduce(f32[40]{0:T(128)S(1)} %reduce_max.9), channel_id=1, replica_groups=mesh['dp'=4,'vocab'=8] {'vocab'}, use_global_device_ids=true, to_apply=%region_4.5 | all-reduce | flops 40 | bytes 320 | tf_op jit(solution)/shard_map/pmax | solution.py:32
  92.7 1.2 %exponential_reduce_fusion = (f32[40]{0:T(128)S(1)}, f32[40]{0:T(128)S(1)}) fusion(f32[40,2020]{1,0:T(8,128)} %reduce-scatter.4.cloned.1.call-done, f32[40]{0:T(128)S(1)} %pmax.7, s32[40]{0:T(128)S(1)} %broadcast_subtract_fusion), kind=kLoop, calls=%fused_computation | loop fusion | flops 403920 | bytes 323840 | tf_op jit(solution)/shard_map/reduce_sum | solution.py:33
  93.9 13.6 %all-reduce.2 = (f32[40]{0:T(128)S(1)}, f32[40]{0:T(128)S(1)}) all-reduce(f32[40]{0:T(128)S(1)} %get-tuple-element.3, f32[40]{0:T(128)S(1)} %get-tuple-element.2), channel_id=1, replica_groups=mesh['dp'=4,'vocab'=8] {'vocab'}, use_global_device_ids=true, to_apply=%region_2.3 | all-reduce | flops 80 | bytes 640 | tf_op jit(solution)/shard_map/psum | solution.py:34
  107.5 0.1 dynamic_slice.3
  107.6 0.0 copy-start.2
  107.6 0.6 slice.7
  108.9 0.0 copy-done.2
  (3 shorter events, 0.0 us)
Async XLA Ops:
  7.2 68.3 %reduce-scatter.4.cloned.1.call-start = ((), (), s32[]{:S(2)}) async-start(), calls=%async_computation.2 | async-start | bytes 1638400
  25.7 21.7 %copy-start.1 = (u32[32]{0:T(128)S(1)}, u32[32]{0:T(128)}, u32[]{:S(2)}) copy-start(u32[32]{0:T(128)} %constant.26) | copy-start | bytes 388
  25.7 23.0 %copy-start = (s32[4]{0:T(128)S(1)}, s32[4]{0:T(128)}, u32[]{:S(2)}) copy-start(s32[4]{0:T(128)} %param.9) | copy-start | bytes 52
  107.6 1.2 %copy-start.2 = (f32[5]{0:T(128)}, f32[5]{0:T(128)S(1)}, u32[]{:S(2)}) copy-start(f32[5]{0:T(128)S(1)} %dynamic_slice.3) | copy-start | bytes 64
Sparse Core Ops, SparseCore 0:
  46.3 29.0 reduce-scatter.3
where the time goes:
time: 117 us
  blocking collectives  70 us (60%)
  between operations  17.8 us (15%)
  waiting for transfers between devices  17.2 us (15%)
  matrix products  6.57 us (6%)
  other arithmetic  3.42 us (3%)
  local copies, waits for them, and re-layouts  1.78 us (2%)
    all_gather x1, blocking collectives, body(): lax.all_gather(hidden, 'vocab', axis=0, tiled=True)  17.6 us
    unnamed x2, waiting for transfers between devices  17.2 us
    pmax x1, blocking collectives, body(): row_top = lax.pmax(local_top, 'vocab')  16.2 us
    psum x1, blocking collectives, body(): totals, picked = lax.psum((local_total, local_picked), 'vocab')  13.6 us
    all_to_all x1, blocking collectives, body(): lax.all_to_all(group_hidden, 'dp', split_axis=1, concat_axis=0, tiled=True)  13.3 us
    unnamed x1, blocking collectives  9.29 us
    dot_general x1, matrix products, body(): jnp.dot(every_rows, lm_head, preferred_element_type=jnp.float32)  6.57 us
  transfers between devices with their start and end apart: 1, of which 1 were waited for; matrix products, arithmetic and copies ran while one was open for 1% of the time, Pallas kernels for 0%

commit v1 on v0

v1 whole, which is shorter than its diff:
```python
import functools

import jax
import jax.numpy as jnp
from jax import lax
from jax.experimental import pallas as pl
from jax.experimental.pallas import tpu as pltpu
from jax.sharding import PartitionSpec as P


BASE = 128
WIRE = jnp.int16
MOST = 32000.0
TINY = 1e-30
CHUNKS = 1
TILES = 4
BLOCK = 16
VMEM = pl.BlockSpec(memory_space=pltpu.VMEM)
SMEM = pl.BlockSpec(memory_space=pltpu.SMEM)
HBM = pl.BlockSpec(memory_space=pltpu.HBM)
F32, BF16 = jnp.float32, jnp.bfloat16


def call(kernel, outs, *args, specs, scratch=(), limit=8 << 20, flops=0, moved=0):
    return pl.pallas_call(
        kernel,
        out_shape=outs,
        in_specs=specs,
        out_specs=jax.tree.map(lambda _: VMEM, outs),
        scratch_shapes=scratch,
        compiler_params=pltpu.CompilerParams(vmem_limit_bytes=limit),
        cost_estimate=pl.CostEstimate(flops=flops, bytes_accessed=moved, transcendentals=0),
    )(*args)


def far(x):
    return pltpu.with_memory_space_constraint(x, pltpu.HBM)


def shape(dims, dtype):
    return jax.ShapeDtypeStruct(dims, dtype)


def sublane(block):
    return lax.broadcasted_iota(jnp.int32, block, 0)


def spread(rows, block):
    out = jnp.zeros(block, F32)
    for i, row in rows.items():
        out = jnp.where(sublane(block) == i, jnp.broadcast_to(row, block), out)
    return out


def part(pre_ref, dec_ref, index):
    quarter = pre_ref.shape[1] // 4
    start = pl.multiple_of(index * quarter, 128)
    return pre_ref[:, pl.ds(start, quarter)].astype(F32), dec_ref[:, pl.ds(start, quarter)].astype(F32)


def load_kernel(pre_hbm, dec_hbm, pre_ref, dec_ref, *refs):
    outs, sems = refs[:-1], refs[-1]
    copies = [
        pltpu.make_async_copy(pre_hbm, pre_ref, sems.at[0]),
        pltpu.make_async_copy(dec_hbm, dec_ref, sems.at[1]),
    ]
    for c in copies:
        c.start()
    for c in copies:
        c.wait()
    me = lax.axis_index("dp")
    for k, out_ref in enumerate(outs, start=1):
        pre, dec = part(pre_ref, dec_ref, me ^ k)
        half = pre.shape[1] // 2
        out_ref[:, :half] = jnp.concatenate([pre[:, :half], pre[:, half:]], axis=0).astype(BF16)
        out_ref[:, half:] = fold(dec).astype(BF16)


def fold(row):
    each = -(-row.shape[1] // 1024) * 128
    rows = {}
    for i in range(8):
        low, high = min(i * each, row.shape[1]), min((i + 1) * each, row.shape[1])
        if high > low:
            rows[i] = row[:, low:high]
            if high - low < each:
                rows[i] = jnp.concatenate([rows[i], jnp.zeros((1, each - high + low), row.dtype)], axis=1)
    return spread(rows, (8, each))


def unfold(block, width):
    return jnp.concatenate([block[i : i + 1] for i in range(8)], axis=1)[:, :width]


def ids_kernel(pre, pt_ref, dt_ref, live_ref, ids_ref, live_out):
    lane = lax.broadcasted_iota(jnp.int32, (8, BASE), 1)
    ids = jnp.zeros((8, BASE), jnp.int32)
    for i in range(pre):
        ids = jnp.where(sublane(ids.shape) == i, pt_ref[i], ids)
    ids = jnp.where(sublane(ids.shape) == pre, dt_ref[0], ids)
    low, mid, high = ids & (BASE - 1), (ids >> 7) & (BASE - 1), ids >> 14
    ids_ref[...] = jnp.where(lane == 0, low, jnp.where(lane == 1, mid, high)).astype(F32).astype(BF16)
    live_out[...] = jnp.broadcast_to(live_ref[0], live_out.shape)


def dense_kernel(pre_ref, dec_ref, r1, r2, r3, ids_ref, out_ref):
    sets = [part(pre_ref, dec_ref, lax.axis_index("dp"))]
    quarter = sets[0][0].shape[1]
    half = quarter // 2
    for r in (r1, r2, r3):
        pre = r[:, :half].astype(F32)
        sets.append((jnp.concatenate([pre[:4], pre[4:]], axis=1), unfold(r[:, half:].astype(F32), quarter)))
    for pair in range(2):
        both = jnp.concatenate([sets[2 * pair][0], sets[2 * pair + 1][0]], axis=0)
        out_ref[:, pair * quarter : (pair + 1) * quarter] = both.astype(BF16)
    rows = {k + 4 * h: s[1][:, h * half : (h + 1) * half] for k, s in enumerate(sets) for h in range(2)}
    out_ref[:, 2 * quarter : 2 * quarter + half] = spread(rows, (8, half)).astype(BF16)
    out_ref[:, 2 * quarter + half :] = ids_ref[...]


def fetch_kernel(parts, head_hbm, out_ref, sems):
    rows = out_ref.shape[0]
    step = -(-(rows // parts) // 8) * 8
    copies = []
    for i in range(parts):
        block = pl.ds(i * step, min((i + 1) * step, rows) - i * step)
        copies.append(pltpu.make_async_copy(head_hbm.at[block], out_ref.at[block], sems.at[i]))
    for c in copies:
        c.start()
    for c in copies:
        c.wait()


def matmul_kernel(n_dp, pre, voc, *refs):
    head_ref, refs = refs[0], refs[1:]
    n_kv = len(refs) - n_dp - 3
    bufs, refs = refs[:n_kv], refs[n_kv:]
    own_ref, outs, tgt_ref, x_ref, last_ref = refs[0], refs[1:n_dp], refs[n_dp], refs[n_dp + 1], refs[n_dp + 2]
    quarter = head_ref.shape[1]
    half = quarter // 2
    pre_rows = pre * n_kv
    tail = n_dp * pre_rows
    wide = -(-voc // 128) * 128
    step = wide // TILES
    tgt_ref[...] = jnp.zeros_like(tgt_ref)
    for kv, buf in enumerate(bufs):
        for pair in range(2):
            block = buf[:, pair * quarter : (pair + 1) * quarter].astype(F32)
            for j in range(2):
                row = (2 * pair + j) * pre_rows + pre * kv
                x_ref[row : row + pre, :] = block[pre * j : pre * (j + 1)]
        block = buf[:, 2 * quarter : 2 * quarter + half].astype(F32)
        for k in range(n_dp):
            row = tail + n_kv * k + kv
            x_ref[row : row + 1, :half] = block[k : k + 1]
            x_ref[row : row + 1, half:] = block[n_dp + k : n_dp + k + 1]
        digits = buf[:, 2 * quarter + half :].astype(F32)
        tgt_ref[pre * kv : pre * (kv + 1), :] = digits[:pre]
        tgt_ref[pre_rows + kv : pre_rows + kv + 1, :] = digits[pre : pre + 1]
    x = x_ref[...].astype(BF16)
    powers = []
    decs = []
    for t in range(TILES):
        start, stop = t * step, min((t + 1) * step, voc)
        y = lax.dot_general(
            x, head_ref[start:stop, :], (((1,), (1,)), ((), ())), preferred_element_type=F32
        )
        own_ref[:pre_rows, start:stop] = y[:pre_rows]
        own_ref[pre_rows : pre_rows + n_kv, start:stop] = y[tail : tail + n_kv]
        most = jnp.maximum(jnp.max(jnp.abs(y), axis=1, keepdims=True), TINY)
        power = jnp.ceil(jnp.log2(most * (1.0 / MOST)))
        powers.append(power)
        code = jnp.round(y * jnp.exp2(-power))
        if t == TILES - 1:
            last_ref[:, : stop - start] = code
            for i, p in enumerate(powers):
                last_ref[:, stop - start + i : stop - start + i + 1] = p
            code = last_ref[...]
        code = code.astype(jnp.int32)
        decs.append(code[tail:])
        for k in range(1, n_dp):
            for g in range(pre_rows // 8):
                low = k * pre_rows + 8 * g
                outs[k - 1][:, g * wide + start : g * wide + start + step] = code[low : low + 8].astype(WIRE)
    folds = 8 // n_kv
    for t in range(TILES // folds):
        for k in range(1, n_dp):
            both = [decs[t + f * (TILES // folds)][n_kv * k : n_kv * (k + 1)] for f in range(folds)]
            col = (pre_rows // 8) * wide + t * step
            outs[k - 1][:, col : col + step] = jnp.concatenate(both, axis=0).astype(WIRE)


def stats_kernel(pre, voc, chunks, *refs):
    out_ref, tile_ref = refs[-2:]
    tile_ref[...] = jnp.zeros_like(tile_ref)
    offset = lax.axis_index("vocab") * voc
    wide = -(-voc // 128) * 128
    step = wide // TILES
    spare = voc - (TILES - 1) * step
    for c in range(chunks):
        own_ref, *parts, tgt_ref = refs[5 * c : 5 * c + 5]
        n_kv = 8 // chunks
        pre_rows = pre * n_kv
        groups = pre_rows // 8

        def logits(piece, own):
            powers = [piece(p, TILES - 1)[:, spare : spare + TILES] for p in parts]
            tiles = []
            for t in range(TILES):
                stop = min(step, voc - t * step)
                total = own[:, t * step : t * step + stop]
                for p, power in zip(parts, powers):
                    total = total + piece(p, t)[:, :stop] * jnp.exp2(power[:, t : t + 1])
                tiles.append(total)
            return jnp.concatenate(tiles, axis=1)

        def pre_piece(g):
            return lambda p, t: p[:, g * wide + t * step : g * wide + (t + 1) * step].astype(F32)

        def dec_piece(p, t):
            per = TILES * n_kv // 8
            col = groups * wide + (t % per) * step
            low = n_kv * (t // per)
            return p[:, col : col + step].astype(F32)[low : low + n_kv]

        sets = [(8 * g, logits(pre_piece(g), own_ref[8 * g : 8 * g + 8, :])) for g in range(groups)]
        sets.append((pre_rows, logits(dec_piece, own_ref[pre_rows : pre_rows + n_kv, :])))
        s = jnp.concatenate([v for _, v in sets], axis=0)
        rows = s.shape[0]
        digits = tgt_ref[:rows]
        ids = digits[:, 0:1] + BASE * digits[:, 1:2] + (BASE * BASE) * digits[:, 2:3]
        local = ids.astype(jnp.int32) - offset
        columns = lax.broadcasted_iota(jnp.int32, s.shape, 1)
        top = jnp.max(s, axis=1, keepdims=True)
        total = jnp.sum(jnp.exp(s - top), axis=1, keepdims=True)
        picked = jnp.sum(jnp.where(columns == local, s, 0.0), axis=1, keepdims=True)
        lane = lax.broadcasted_iota(jnp.int32, (rows, 128), 1)
        st = jnp.where(lane == 0, top, jnp.where(lane == 1, total, picked))
        for kv in range(n_kv):
            at = BLOCK * (4 * (kv // (n_kv // 2)) + n_kv // 2 * c + kv % (n_kv // 2))
            tile_ref[at : at + pre, :] = st[pre * kv : pre * (kv + 1)]
            tile_ref[at + pre : at + pre + 1, :] = st[pre_rows + kv : pre_rows + kv + 1]
    out_ref[...] = jnp.transpose(tile_ref[...])[:8, :]


def merge(a, b):
    top = jnp.maximum(a[0:1], b[0:1])
    total = a[1:2] * jnp.exp(a[0:1] - top) + b[1:2] * jnp.exp(b[0:1] - top)
    return jnp.concatenate([top, total, a[2:3] + b[2:3]], axis=0)


def pair_kernel(mine_ref, other_ref, out_ref):
    other = pltpu.roll(other_ref[...], 64, 1)
    out_ref[0:3, :] = merge(mine_ref[...], other)
    out_ref[3:8, :] = jnp.zeros((5, 128), F32)


def final_kernel(pre, dec, mine_ref, r1, r2, r3, live_ref, pre_ref, dec_ref):
    total = mine_ref[...]
    for k, r in enumerate((r1, r2, r3), start=1):
        total = merge(total, pltpu.roll(r[...], 128 - BLOCK * k, 1))
    value = total[2:3] - (total[0:1] + jnp.log(total[1:2]))
    position = lax.axis_index("vocab") * dec
    pre_ref[...] = value[0, :pre]
    dec_ref[...] = jnp.where(position < live_ref[0, :dec], value[0, pre : pre + dec], 0.0)


def fast_body(n_dp, n_vocab, pre_hidden, dec_hidden, lm_head, pre_targets, dec_targets, dec_live):
    pre, dec = pre_hidden.shape[0], dec_hidden.shape[0]
    quarter, voc = lm_head.shape
    half = quarter // 2

    def swap(x, axis, k):
        return lax.ppermute(x, axis, [(i, i ^ k) for i in range(n_dp if axis == "dp" else n_vocab)])

    fold_width = half + -(-quarter // 1024) * 128
    pre_v, dec_v, *sends = call(
        load_kernel,
        [shape(pre_hidden.shape, BF16), shape(dec_hidden.shape, BF16)] + [shape((8, fold_width), BF16)] * (n_dp - 1),
        far(pre_hidden),
        far(dec_hidden),
        specs=[HBM] * 2,
        scratch=[pltpu.SemaphoreType.DMA((2,))],
    )
    ids, live = call(
        functools.partial(ids_kernel, pre),
        [shape((8, BASE), BF16), shape((1, 128), jnp.int32)],
        pre_targets,
        dec_targets,
        dec_live,
        specs=[SMEM] * 3,
    )
    wide = -(-voc // 128) * 128
    head = call(
        functools.partial(fetch_kernel, 8),
        shape((voc, quarter), BF16),
        far(lm_head.T),
        specs=[HBM],
        scratch=[pltpu.SemaphoreType.DMA((8,))],
        moved=4 * quarter * voc,
    )
    got = [swap(s, "dp", k) for k, s in enumerate(sends, start=1)]
    mine = call(dense_kernel, shape((8, 2 * quarter + half + BASE), BF16), pre_v, dec_v, *got, ids, specs=[VMEM] * 6)
    chips = [mine] + [swap(mine, "vocab", 2 * k) for k in (1, 2, 3)]
    cores = [swap(b, "vocab", 1) for b in chips]

    operands = []
    for c in range(CHUNKS):
        per = 4 // CHUNKS
        bufs = chips[per * c : per * (c + 1)] + cores[per * c : per * (c + 1)]
        group = len(bufs) * (pre + dec)
        rows = n_dp * group
        piece = shape((8, group * wide // 8), WIRE)
        own, *parts, tgt = call(
            functools.partial(matmul_kernel, n_dp, pre, voc),
            [shape((-(-group // 8) * 8, voc), F32)] + [piece] * (n_dp - 1) + [shape((-(-group // 8) * 8, BASE), F32)],
            head,
            *bufs,
            specs=[VMEM] * (1 + len(bufs)),
            scratch=[pltpu.VMEM((rows, quarter), F32), pltpu.VMEM((rows, wide // TILES), F32)],
            limit=16 << 20,
            flops=2 * rows * quarter * voc,
        )
        operands += [own] + [swap(p, "dp", k) for k, p in enumerate(parts, start=1)] + [tgt]
    stats = call(
        functools.partial(stats_kernel, pre, voc, CHUNKS),
        shape((8, 128), F32),
        *operands,
        specs=[VMEM] * len(operands),
        scratch=[pltpu.VMEM((128, 128), F32)],
    )
    both = call(pair_kernel, shape((8, 128), F32), stats, swap(stats, "vocab", 1), specs=[VMEM] * 2)
    others = [swap(both, "vocab", 2 * k) for k in (1, 2, 3)]
    return tuple(
        call(
            functools.partial(final_kernel, pre, dec),
            [shape((pre,), F32), shape((dec,), F32)],
            both,
            *others,
            live,
            specs=[VMEM] * 5,
        )
    )


def plain_body(pre_hidden, dec_hidden, lm_head, pre_targets, dec_targets, dec_live):
    pre, dec = pre_hidden.shape[0], dec_hidden.shape[0]
    own = pre + dec
    voc = lm_head.shape[1]
    hidden = jnp.concatenate([pre_hidden, dec_hidden], axis=0)
    targets = jnp.concatenate([pre_targets, dec_targets], axis=0)
    me = lax.axis_index("vocab")
    group_hidden = lax.all_gather(hidden, "vocab", axis=0, tiled=True)
    group_targets = lax.all_gather(targets, "vocab", axis=0, tiled=True)
    every = lax.all_to_all(group_hidden, "dp", split_axis=1, concat_axis=0, tiled=True)
    partial = jnp.dot(every, lm_head, preferred_element_type=F32)
    logits = lax.psum_scatter(partial, "dp", scatter_dimension=0, tiled=True)
    hit = (group_targets - me * voc)[:, None] == jnp.arange(voc, dtype=jnp.int32)[None, :]
    picked = jnp.sum(jnp.where(hit, logits, 0.0), axis=1)
    top = lax.pmax(jnp.max(logits, axis=1), "vocab")
    total = jnp.sum(jnp.exp(logits - top[:, None]), axis=1)
    total, picked = lax.psum((total, picked), "vocab")
    values = lax.dynamic_slice_in_dim(picked - (top + jnp.log(total)), me * own, own, 0)
    positions = me * dec + jnp.arange(dec, dtype=jnp.int32)
    return values[:pre], jnp.where(positions < dec_live[0], values[pre:], 0.0)


def solution(mesh):
    n_dp, n_vocab = mesh.shape["dp"], mesh.shape["vocab"]

    def body(pre_hidden, dec_hidden, lm_head, *rest):
        quarter, voc = lm_head.shape
        fits = (n_dp, n_vocab, pre_hidden.shape[0], dec_hidden.shape[0]) == (4, 8, 4, 1)
        fits = fits and quarter % 256 == 0 and TILES <= -voc % 128 and -(-voc // 128) % TILES == 0
        run = functools.partial(fast_body, n_dp, n_vocab) if fits else plain_body
        return run(pre_hidden, dec_hidden, lm_head, *rest)

    rows = P(("dp", "vocab"))
    in_specs = (P(("dp", "vocab"), None), P(("dp", "vocab"), None), P("dp", "vocab"), rows, rows, P("dp"))
    return jax.shard_map(body, mesh=mesh, in_specs=in_specs, out_specs=(rows, rows), check_vma=False)
```

time: 117 us -> 45.4 us (0.39)
  blocking collectives: 70 us -> 0 us
  starting transfers between devices: 0.04 us -> 17.5 us
  between operations: 17.8 us -> 2.04 us
  Pallas kernels: 0 us -> 8.49 us
  matrix products: 6.57 us -> 0 us
  other arithmetic: 3.42 us -> 0 us
    all_gather x1 -> x0, blocking collectives: 17.6 us -> none  [body(): lax.all_gather(hidden, 'vocab', axis=0, tiled=True)]
    ppermute x0 -> x17, starting transfers between devices: none -> 17.5 us  [swap(): lax.ppermute(x, axis, [(i, i ^ k) for i in range(n_dp if axis == 'dp' els...]
    unnamed x2 -> x0, waiting for transfers between devices: 17.2 us -> none
    ppermute x0 -> x17, waiting for transfers between devices: none -> 16.4 us  [swap(): lax.ppermute(x, axis, [(i, i ^ k) for i in range(n_dp if axis == 'dp' els...]
    pmax x1 -> x0, blocking collectives: 16.2 us -> none  [body(): row_top = lax.pmax(local_top, 'vocab')]
    psum x1 -> x0, blocking collectives: 13.6 us -> none  [body(): totals, picked = lax.psum((local_total, local_picked), 'vocab')]
    all_to_all x1 -> x0, blocking collectives: 13.3 us -> none  [body(): lax.all_to_all(group_hidden, 'dp', split_axis=1, concat_axis=0, tiled=True)]
    unnamed x1 -> x0, blocking collectives: 9.29 us -> none
  transfers between devices with their start and end apart: 1 -> 17, of which waited for: 1 -> 8; matrix products, arithmetic and copies ran while one was open for 1% -> 0% of each run, Pallas kernels for 0% -> 8%
where the time goes in v1:
time: 45.4 us; the launch traced here: 45.2 us
  starting transfers between devices  17.5 us (39%)
  waiting for transfers between devices  16.4 us (36%)
  Pallas kernels  8.49 us (19%)
  between operations  2.04 us (4%)
  local copies, waits for them, and re-layouts  0.65 us (1%)
    ppermute x17, starting transfers between devices, swap(): lax.ppermute(x, axis, [(i, i ^ k) for i in range(n_dp if axis == 'dp' els...  17.5 us
    ppermute x17, waiting for transfers between devices, swap(): lax.ppermute(x, axis, [(i, i ^ k) for i in range(n_dp if axis == 'dp' els...  16.4 us
    pallas_call x8, Pallas kernels, call(): pl.pallas_call(kernel, out_shape=outs, in_specs=specs, out_specs=jax.tree...  8.49 us
  transfers between devices with their start and end apart: 17, of which 8 were waited for; matrix products, arithmetic and copies ran while one was open for 0% of the time, Pallas kernels for 8%

profile of v1, /device:TPU:0, one launch (start us, length us, event | category | flops | bytes accessed | tf_op | source)
XLA Modules:
  0.0 45.2 jit_solution(1651645496939876476)
XLA Ops:
  0.6 0.9 %shard_map.78 = (bf16[4,7168]{1,0:T(4,128)(2,1)S(1)}, bf16[1,7168]{1,0:T(2,128)(2,1)S(1)}, bf16[8,1152]{1,0:T(8,128)(2,1)S(1)}, bf16[8,1152]{1,0:T(8,128)(2,1)S(1)}, bf16[8,1152]{1,0:T(8,128)(2,1)S(1)}) custom-call(bf16[4,7168]{1,0:T(4,128)(2,1)} %pre_hbm.1, bf16[1,7168]{1,0:T(2,128)(2,1)} %dec_hbm.1), custom_call_target="tpu_custom_call" | custom-call | tf_op jit(solution)/shard_map/pallas_call | solution.py:25
  1.5 3.0 %collective-permute-start = (bf16[8,1152]{1,0:T(8,128)(2,1)S(1)}, bf16[8,1152]{1,0:T(8,128)(2,1)S(1)}, u32[]{:S(2)}, u32[]{:S(2)}) collective-permute-start(bf16[8,1152]{1,0:T(8,128)(2,1)S(1)} %get-tuple-element.16), channel_id=1, source_target_pairs={{0,8},{8,0},{16,24},{24,16},{1,9},{9,1},{17,25},{25,17},{2,10},{10... | collective-permute-start | bytes 55304 | tf_op jit(solution)/shard_map/ppermute | solution.py:274
  4.5 1.5 %collective-permute-start.1 = (bf16[8,1152]{1,0:T(8,128)(2,1)S(1)}, bf16[8,1152]{1,0:T(8,128)(2,1)S(1)}, u32[]{:S(2)}, u32[]{:S(2)}) collective-permute-start(bf16[8,1152]{1,0:T(8,128)(2,1)S(1)} %get-tuple-element.17), channel_id=1, source_target_pairs={{0,16},{8,24},{16,0},{24,8},{1,17},{9,25},{17,1},{25,9},{2,18},{10... | collective-permute-start | bytes 55304 | tf_op jit(solution)/shard_map/ppermute | solution.py:274
  6.1 0.0 collective-permute-start.2
  7.4 0.0 copy-start
  7.4 0.6 %copy-done = s32[4]{0:T(128)S(1)} copy-done((s32[4]{0:T(128)S(1)}, s32[4]{0:T(128)}, u32[]{:S(2)}) %copy-start) | copy-done | bytes 40
  8.0 0.6 %shard_map.79 = (bf16[8,128]{1,0:T(8,128)(2,1)S(1)}, s32[1,128]{1,0:T(1,128)S(1)}) custom-call(s32[4]{0:T(128)S(1)} %copy-done, s32[1]{0:T(128)S(6)} %copy.8.dt_ref, s32[1]{0:T(128)S(6)} %copy.9.live_ref), custom_call_target="tpu_custom_call" | custom-call | tf_op jit(solution)/shard_map/pallas_call | solution.py:25
  8.6 0.0 collective-permute-done.r1
  8.6 0.0 collective-permute-done.1.r2
  8.6 2.1 %collective-permute-done.2.r3 = bf16[8,1152]{1,0:T(8,128)(2,1)S(1)} collective-permute-done((bf16[8,1152]{1,0:T(8,128)(2,1)S(1)}, bf16[8,1152]{1,0:T(8,128)(2,1)S(1)}, u32[]{:S(2)}, u32[]{:S(2)}) %collective-permute-start.2) | collective-permute-done | bytes 18464 | tf_op jit(solution)/shard_map/ppermute | solution.py:274
  10.8 3.7 %collective-permute-start.5 = (bf16[8,4608]{1,0:T(8,128)(2,1)S(1)}, bf16[8,4608]{1,0:T(8,128)(2,1)S(1)}, u32[]{:S(2)}, u32[]{:S(2)}) collective-permute-start(bf16[8,4608]{1,0:T(8,128)(2,1)S(1)} %shard_map.80.refs_1_), channel_id=1, source_target_pairs={{0,6},{1,7},{2,4},{3,5},{4,2},{5,3},{6,0},{7,1},{8,14},{9,15},{10,... | collective-permute-start | bytes 221192 | tf_op jit(solution)/shard_map/ppermute | solution.py:274
  14.4 0.0 collective-permute-start.4
  14.4 0.8 %collective-permute-start.3 = (bf16[8,4608]{1,0:T(8,128)(2,1)S(1)}, bf16[8,4608]{1,0:T(8,128)(2,1)S(1)}, u32[]{:S(2)}, u32[]{:S(2)}) collective-permute-start(bf16[8,4608]{1,0:T(8,128)(2,1)S(1)} %shard_map.80.refs_1_), channel_id=1, source_target_pairs={{0,2},{1,3},{2,0},{3,1},{4,6},{5,7},{6,4},{7,5},{8,10},{9,11},{10,... | collective-permute-start | bytes 221192 | tf_op jit(solution)/shard_map/ppermute | solution.py:274
  15.2 0.0 collective-permute-start.6
  15.2 1.9 %collective-permute-done.5.refs_4_ = bf16[8,4608]{1,0:T(8,128)(2,1)S(1)} collective-permute-done((bf16[8,4608]{1,0:T(8,128)(2,1)S(1)}, bf16[8,4608]{1,0:T(8,128)(2,1)S(1)}, u32[]{:S(2)}, u32[]{:S(2)}) %collective-permute-start.5) | collective-permute-done | bytes 73760 | tf_op jit(solution)/shard_map/ppermute | solution.py:274
  17.1 0.0 collective-permute-start.9
  17.1 2.6 %collective-permute-done.4.refs_3_ = bf16[8,4608]{1,0:T(8,128)(2,1)S(1)} collective-permute-done((bf16[8,4608]{1,0:T(8,128)(2,1)S(1)}, bf16[8,4608]{1,0:T(8,128)(2,1)S(1)}, u32[]{:S(2)}, u32[]{:S(2)}) %collective-permute-start.4) | collective-permute-done | bytes 73760 | tf_op jit(solution)/shard_map/ppermute | solution.py:274
  19.7 0.0 collective-permute-start.8
  19.7 0.0 collective-permute-done.3.refs_2_
  19.7 0.5 %collective-permute-start.7 = (bf16[8,4608]{1,0:T(8,128)(2,1)S(1)}, bf16[8,4608]{1,0:T(8,128)(2,1)S(1)}, u32[]{:S(2)}, u32[]{:S(2)}) collective-permute-start(bf16[8,4608]{1,0:T(8,128)(2,1)S(1)} %collective-permute-done.3.refs_2_), channel_id=1, source_target_pairs={{0,1},{1,0},{2,3},{3,2},{4,5},{5,4},{6,7},{7,6},{8,9},{9,8},{10,11... | collective-permute-start | bytes 221192 | tf_op jit(solution)/shard_map/ppermute | solution.py:274
  20.2 3.1 %shard_map.77.refs_0_ = bf16[2020,1792]{1,0:T(8,128)(2,1)S(1)} custom-call(bf16[2020,1792]{1,0:T(8,128)(2,1)} %bitcast.1), custom_call_target="tpu_custom_call" | custom-call | bytes 14479360 | tf_op jit(solution)/shard_map/pallas_call | solution.py:25
  23.4 0.0 collective-permute-done.6.refs_5_
  23.4 0.0 collective-permute-done.9.refs_8_
  23.4 0.0 collective-permute-done.8.refs_7_
  23.4 0.0 collective-permute-done.7.refs_6_
  23.4 2.7 %shard_map.81 = (f32[40,2020]{1,0:T(8,128)S(1)}, s16[8,10240]{1,0:T(8,128)(2,1)S(1)}, s16[8,10240]{1,0:T(8,128)(2,1)S(1)}, s16[8,10240]{1,0:T(8,128)(2,1)S(1)}, f32[40,128]{1,0:T(8,128)S(1)}) custom-call(bf16[2020,1792]{1,0:T(8,128)(2,1)S(1)} %shard_map.77.refs_0_, bf16[8,4608]{1,0:T(8,128)(2,1)S(1)} %shard_map.80.refs_1_, ...), custom_call_target="tpu_custom_call" | custom-call | flops 1158348800 | tf_op jit(solution)/shard_map/pallas_call | solution.py:25
  26.1 0.7 %collective-permute-start.10 = (s16[8,10240]{1,0:T(8,128)(2,1)S(1)}, s16[8,10240]{1,0:T(8,128)(2,1)S(1)}, u32[]{:S(2)}, u32[]{:S(2)}) collective-permute-start(s16[8,10240]{1,0:T(8,128)(2,1)S(1)} %get-tuple-element.21), channel_id=1, source_target_pairs={{0,8},{8,0},{16,24},{24,16},{1,9},{9,1},{17,25},{25,17},{2,10},{10... | collective-permute-start | bytes 491528 | tf_op jit(solution)/shard_map/ppermute | solution.py:274
  26.7 1.2 %collective-permute-start.11 = (s16[8,10240]{1,0:T(8,128)(2,1)S(1)}, s16[8,10240]{1,0:T(8,128)(2,1)S(1)}, u32[]{:S(2)}, u32[]{:S(2)}) collective-permute-start(s16[8,10240]{1,0:T(8,128)(2,1)S(1)} %get-tuple-element.22), channel_id=1, source_target_pairs={{0,16},{8,24},{16,0},{24,8},{1,17},{9,25},{17,1},{25,9},{2,18},{10... | collective-permute-start | bytes 491528 | tf_op jit(solution)/shard_map/ppermute | solution.py:274
  28.0 1.6 %collective-permute-start.12 = (s16[8,10240]{1,0:T(8,128)(2,1)S(1)}, s16[8,10240]{1,0:T(8,128)(2,1)S(1)}, u32[]{:S(2)}, u32[]{:S(2)}) collective-permute-start(s16[8,10240]{1,0:T(8,128)(2,1)S(1)} %get-tuple-element.23), channel_id=1, source_target_pairs={{0,24},{8,16},{16,8},{24,0},{1,25},{9,17},{17,9},{25,1},{2,26},{10... | collective-permute-start | bytes 491528 | tf_op jit(solution)/shard_map/ppermute | solution.py:274
  29.6 3.6 %collective-permute-done.10.refs_1_ = s16[8,10240]{1,0:T(8,128)(2,1)S(1)} collective-permute-done((s16[8,10240]{1,0:T(8,128)(2,1)S(1)}, s16[8,10240]{1,0:T(8,128)(2,1)S(1)}, u32[]{:S(2)}, u32[]{:S(2)}) %collective-permute-start.10) | collective-permute-done | bytes 163872 | tf_op jit(solution)/shard_map/ppermute | solution.py:274
  33.2 2.9 %collective-permute-done.11.refs_2_ = s16[8,10240]{1,0:T(8,128)(2,1)S(1)} collective-permute-done((s16[8,10240]{1,0:T(8,128)(2,1)S(1)}, s16[8,10240]{1,0:T(8,128)(2,1)S(1)}, u32[]{:S(2)}, u32[]{:S(2)}) %collective-permute-start.11) | collective-permute-done | bytes 163872 | tf_op jit(solution)/shard_map/ppermute | solution.py:274
  36.1 0.0 collective-permute-done.12.refs_3_
  36.1 0.4 shard_map.82.mine_ref
  36.5 0.0 collective-permute-start.13
  36.6 1.2 %collective-permute-done.13.other_ref = f32[8,128]{1,0:T(8,128)S(1)} collective-permute-done((f32[8,128]{1,0:T(8,128)S(1)}, f32[8,128]{1,0:T(8,128)S(1)}, u32[]{:S(2)}, u32[]{:S(2)}) %collective-permute-start.13) | collective-permute-done | bytes 4128 | tf_op jit(solution)/shard_map/ppermute | solution.py:274
  37.7 0.1 shard_map.83.mine_ref
  37.8 2.1 %collective-permute-start.16 = (f32[8,128]{1,0:T(8,128)S(1)}, f32[8,128]{1,0:T(8,128)S(1)}, u32[]{:S(2)}, u32[]{:S(2)}) collective-permute-start(f32[8,128]{1,0:T(8,128)S(1)} %shard_map.83.mine_ref), channel_id=1, source_target_pairs={{0,6},{1,7},{2,4},{3,5},{4,2},{5,3},{6,0},{7,1},{8,14},{9,15},{10,... | collective-permute-start | bytes 12296 | tf_op jit(solution)/shard_map/ppermute | solution.py:274
  39.9 0.0 collective-permute-start.15
  39.9 2.3 %collective-permute-start.14 = (f32[8,128]{1,0:T(8,128)S(1)}, f32[8,128]{1,0:T(8,128)S(1)}, u32[]{:S(2)}, u32[]{:S(2)}) collective-permute-start(f32[8,128]{1,0:T(8,128)S(1)} %shard_map.83.mine_ref), channel_id=1, source_target_pairs={{0,2},{1,3},{2,0},{3,1},{4,6},{5,7},{6,4},{7,5},{8,10},{9,11},{10,... | collective-permute-start | bytes 12296 | tf_op jit(solution)/shard_map/ppermute | solution.py:274
  42.2 1.0 %collective-permute-done.16.r3 = f32[8,128]{1,0:T(8,128)S(1)} collective-permute-done((f32[8,128]{1,0:T(8,128)S(1)}, f32[8,128]{1,0:T(8,128)S(1)}, u32[]{:S(2)}, u32[]{:S(2)}) %collective-permute-start.16) | collective-permute-done | bytes 4128 | tf_op jit(solution)/shard_map/ppermute | solution.py:274
  43.2 1.2 %collective-permute-done.15.r2 = f32[8,128]{1,0:T(8,128)S(1)} collective-permute-done((f32[8,128]{1,0:T(8,128)S(1)}, f32[8,128]{1,0:T(8,128)S(1)}, u32[]{:S(2)}, u32[]{:S(2)}) %collective-permute-start.15) | collective-permute-done | bytes 4128 | tf_op jit(solution)/shard_map/ppermute | solution.py:274
  44.5 0.0 collective-permute-done.14.r1
  44.5 0.7 %shard_map.84 = (f32[4]{0:T(128)}, f32[1]{0:T(128)}) custom-call(f32[8,128]{1,0:T(8,128)S(1)} %shard_map.83.mine_ref, f32[8,128]{1,0:T(8,128)S(1)} %collective-permute-done.14.r1, f32[8,128]{1,0:T(8,128)S(1)} %collective-permute-done.15.r2, f32[8,128]{1,0:T(8,128)S(1)} %collective-permute-done.16.r3, s32[1,128]{1,0:T(1,128)S(1)} %get-tuple-element.25.live_ref), custom_call_target="tpu_custom_call" | custom-call | tf_op jit(solution)/shard_map/pallas_call | solution.py:25
  (1 shorter events, 0.0 us)
Async XLA Ops:
  1.5 7.1 %collective-permute-start = (bf16[8,1152]{1,0:T(8,128)(2,1)S(1)}, bf16[8,1152]{1,0:T(8,128)(2,1)S(1)}, u32[]{:S(2)}, u32[]{:S(2)}) collective-permute-start(bf16[8,1152]{1,0:T(8,128)(2,1)S(1)} %get-tuple-element.16), channel_id=1, source_target_pairs={{0,8},{8,0},{16,24},{24,16},{1,9},{9,1},{17,25},{25,17},{2,10},{10... | collective-permute-start | bytes 55304 | tf_op jit(solution)/shard_map/ppermute | solution.py:274
  4.5 4.1 %collective-permute-start.1 = (bf16[8,1152]{1,0:T(8,128)(2,1)S(1)}, bf16[8,1152]{1,0:T(8,128)(2,1)S(1)}, u32[]{:S(2)}, u32[]{:S(2)}) collective-permute-start(bf16[8,1152]{1,0:T(8,128)(2,1)S(1)} %get-tuple-element.17), channel_id=1, source_target_pairs={{0,16},{8,24},{16,0},{24,8},{1,17},{9,25},{17,1},{25,9},{2,18},{10... | collective-permute-start | bytes 55304 | tf_op jit(solution)/shard_map/ppermute | solution.py:274
  6.1 4.7 %collective-permute-start.2 = (bf16[8,1152]{1,0:T(8,128)(2,1)S(1)}, bf16[8,1152]{1,0:T(8,128)(2,1)S(1)}, u32[]{:S(2)}, u32[]{:S(2)}) collective-permute-start(bf16[8,1152]{1,0:T(8,128)(2,1)S(1)} %get-tuple-element.18), channel_id=1, source_target_pairs={{0,24},{8,16},{16,8},{24,0},{1,25},{9,17},{17,9},{25,1},{2,26},{10... | collective-permute-start | bytes 55304 | tf_op jit(solution)/shard_map/ppermute | solution.py:274
  7.4 0.7 %copy-start = (s32[4]{0:T(128)S(1)}, s32[4]{0:T(128)}, u32[]{:S(2)}) copy-start(s32[4]{0:T(128)} %pt_ref.1) | copy-start | bytes 52
  10.8 6.3 %collective-permute-start.5 = (bf16[8,4608]{1,0:T(8,128)(2,1)S(1)}, bf16[8,4608]{1,0:T(8,128)(2,1)S(1)}, u32[]{:S(2)}, u32[]{:S(2)}) collective-permute-start(bf16[8,4608]{1,0:T(8,128)(2,1)S(1)} %shard_map.80.refs_1_), channel_id=1, source_target_pairs={{0,6},{1,7},{2,4},{3,5},{4,2},{5,3},{6,0},{7,1},{8,14},{9,15},{10,... | collective-permute-start | bytes 221192 | tf_op jit(solution)/shard_map/ppermute | solution.py:274
  14.4 5.3 %collective-permute-start.4 = (bf16[8,4608]{1,0:T(8,128)(2,1)S(1)}, bf16[8,4608]{1,0:T(8,128)(2,1)S(1)}, u32[]{:S(2)}, u32[]{:S(2)}) collective-permute-start(bf16[8,4608]{1,0:T(8,128)(2,1)S(1)} %shard_map.80.refs_1_), channel_id=1, source_target_pairs={{0,4},{1,5},{2,6},{3,7},{4,0},{5,1},{6,2},{7,3},{8,12},{9,13},{10,... | collective-permute-start | bytes 221192 | tf_op jit(solution)/shard_map/ppermute | solution.py:274
  14.4 5.3 %collective-permute-start.3 = (bf16[8,4608]{1,0:T(8,128)(2,1)S(1)}, bf16[8,4608]{1,0:T(8,128)(2,1)S(1)}, u32[]{:S(2)}, u32[]{:S(2)}) collective-permute-start(bf16[8,4608]{1,0:T(8,128)(2,1)S(1)} %shard_map.80.refs_1_), channel_id=1, source_target_pairs={{0,2},{1,3},{2,0},{3,1},{4,6},{5,7},{6,4},{7,5},{8,10},{9,11},{10,... | collective-permute-start | bytes 221192 | tf_op jit(solution)/shard_map/ppermute | solution.py:274
  15.2 8.1 %collective-permute-start.6 = (bf16[8,4608]{1,0:T(8,128)(2,1)S(1)}, bf16[8,4608]{1,0:T(8,128)(2,1)S(1)}, u32[]{:S(2)}, u32[]{:S(2)}) collective-permute-start(bf16[8,4608]{1,0:T(8,128)(2,1)S(1)} %shard_map.80.refs_1_), channel_id=1, source_target_pairs={{0,1},{1,0},{2,3},{3,2},{4,5},{5,4},{6,7},{7,6},{8,9},{9,8},{10,11... | collective-permute-start | bytes 221192 | tf_op jit(solution)/shard_map/ppermute | solution.py:274
  17.1 6.3 %collective-permute-start.9 = (bf16[8,4608]{1,0:T(8,128)(2,1)S(1)}, bf16[8,4608]{1,0:T(8,128)(2,1)S(1)}, u32[]{:S(2)}, u32[]{:S(2)}) collective-permute-start(bf16[8,4608]{1,0:T(8,128)(2,1)S(1)} %collective-permute-done.5.refs_4_), channel_id=1, source_target_pairs={{0,1},{1,0},{2,3},{3,2},{4,5},{5,4},{6,7},{7,6},{8,9},{9,8},{10,11... | collective-permute-start | bytes 221192 | tf_op jit(solution)/shard_map/ppermute | solution.py:274
  19.7 3.7 %collective-permute-start.8 = (bf16[8,4608]{1,0:T(8,128)(2,1)S(1)}, bf16[8,4608]{1,0:T(8,128)(2,1)S(1)}, u32[]{:S(2)}, u32[]{:S(2)}) collective-permute-start(bf16[8,4608]{1,0:T(8,128)(2,1)S(1)} %collective-permute-done.4.refs_3_), channel_id=1, source_target_pairs={{0,1},{1,0},{2,3},{3,2},{4,5},{5,4},{6,7},{7,6},{8,9},{9,8},{10,11... | collective-permute-start | bytes 221192 | tf_op jit(solution)/shard_map/ppermute | solution.py:274
  19.7 3.7 %collective-permute-start.7 = (bf16[8,4608]{1,0:T(8,128)(2,1)S(1)}, bf16[8,4608]{1,0:T(8,128)(2,1)S(1)}, u32[]{:S(2)}, u32[]{:S(2)}) collective-permute-start(bf16[8,4608]{1,0:T(8,128)(2,1)S(1)} %collective-permute-done.3.refs_2_), channel_id=1, source_target_pairs={{0,1},{1,0},{2,3},{3,2},{4,5},{5,4},{6,7},{7,6},{8,9},{9,8},{10,11... | collective-permute-start | bytes 221192 | tf_op jit(solution)/shard_map/ppermute | solution.py:274
  26.1 7.1 %collective-permute-start.10 = (s16[8,10240]{1,0:T(8,128)(2,1)S(1)}, s16[8,10240]{1,0:T(8,128)(2,1)S(1)}, u32[]{:S(2)}, u32[]{:S(2)}) collective-permute-start(s16[8,10240]{1,0:T(8,128)(2,1)S(1)} %get-tuple-element.21), channel_id=1, source_target_pairs={{0,8},{8,0},{16,24},{24,16},{1,9},{9,1},{17,25},{25,17},{2,10},{10... | collective-permute-start | bytes 491528 | tf_op jit(solution)/shard_map/ppermute | solution.py:274
  26.7 9.3 %collective-permute-start.11 = (s16[8,10240]{1,0:T(8,128)(2,1)S(1)}, s16[8,10240]{1,0:T(8,128)(2,1)S(1)}, u32[]{:S(2)}, u32[]{:S(2)}) collective-permute-start(s16[8,10240]{1,0:T(8,128)(2,1)S(1)} %get-tuple-element.22), channel_id=1, source_target_pairs={{0,16},{8,24},{16,0},{24,8},{1,17},{9,25},{17,1},{25,9},{2,18},{10... | collective-permute-start | bytes 491528 | tf_op jit(solution)/shard_map/ppermute | solution.py:274
  28.0 8.1 %collective-permute-start.12 = (s16[8,10240]{1,0:T(8,128)(2,1)S(1)}, s16[8,10240]{1,0:T(8,128)(2,1)S(1)}, u32[]{:S(2)}, u32[]{:S(2)}) collective-permute-start(s16[8,10240]{1,0:T(8,128)(2,1)S(1)} %get-tuple-element.23), channel_id=1, source_target_pairs={{0,24},{8,16},{16,8},{24,0},{1,25},{9,17},{17,9},{25,1},{2,26},{10... | collective-permute-start | bytes 491528 | tf_op jit(solution)/shard_map/ppermute | solution.py:274
  36.5 1.2 %collective-permute-start.13 = (f32[8,128]{1,0:T(8,128)S(1)}, f32[8,128]{1,0:T(8,128)S(1)}, u32[]{:S(2)}, u32[]{:S(2)}) collective-permute-start(f32[8,128]{1,0:T(8,128)S(1)} %shard_map.82.mine_ref), channel_id=1, source_target_pairs={{0,1},{1,0},{2,3},{3,2},{4,5},{5,4},{6,7},{7,6},{8,9},{9,8},{10,11... | collective-permute-start | bytes 12296 | tf_op jit(solution)/shard_map/ppermute | solution.py:274
  37.8 5.4 %collective-permute-start.16 = (f32[8,128]{1,0:T(8,128)S(1)}, f32[8,128]{1,0:T(8,128)S(1)}, u32[]{:S(2)}, u32[]{:S(2)}) collective-permute-start(f32[8,128]{1,0:T(8,128)S(1)} %shard_map.83.mine_ref), channel_id=1, source_target_pairs={{0,6},{1,7},{2,4},{3,5},{4,2},{5,3},{6,0},{7,1},{8,14},{9,15},{10,... | collective-permute-start | bytes 12296 | tf_op jit(solution)/shard_map/ppermute | solution.py:274
  39.9 4.5 %collective-permute-start.15 = (f32[8,128]{1,0:T(8,128)S(1)}, f32[8,128]{1,0:T(8,128)S(1)}, u32[]{:S(2)}, u32[]{:S(2)}) collective-permute-start(f32[8,128]{1,0:T(8,128)S(1)} %shard_map.83.mine_ref), channel_id=1, source_target_pairs={{0,4},{1,5},{2,6},{3,7},{4,0},{5,1},{6,2},{7,3},{8,12},{9,13},{10,... | collective-permute-start | bytes 12296 | tf_op jit(solution)/shard_map/ppermute | solution.py:274
  39.9 4.5 %collective-permute-start.14 = (f32[8,128]{1,0:T(8,128)S(1)}, f32[8,128]{1,0:T(8,128)S(1)}, u32[]{:S(2)}, u32[]{:S(2)}) collective-permute-start(f32[8,128]{1,0:T(8,128)S(1)} %shard_map.83.mine_ref), channel_id=1, source_target_pairs={{0,2},{1,3},{2,0},{3,1},{4,6},{5,7},{6,4},{7,5},{8,10},{9,11},{10,... | collective-permute-start | bytes 12296 | tf_op jit(solution)/shard_map/ppermute | solution.py:274

commit v2 on v1

v2 whole, which is shorter than its diff:
```python
import functools

import jax
import jax.numpy as jnp
from jax import lax
from jax.experimental import pallas as pl
from jax.experimental.pallas import tpu as pltpu
from jax.sharding import PartitionSpec as P


BASE = 128
WIRE = jnp.int16
MOST = 32000.0
TINY = 1e-30
ROWS_CROSS = 1
TILES = 4
BLOCK = 16
VMEM = pl.BlockSpec(memory_space=pltpu.VMEM)
SMEM = pl.BlockSpec(memory_space=pltpu.SMEM)
HBM = pl.BlockSpec(memory_space=pltpu.HBM)
F32, BF16 = jnp.float32, jnp.bfloat16


def call(kernel, outs, *args, specs, scratch=(), limit=8 << 20, flops=0, moved=0):
    return pl.pallas_call(
        kernel,
        out_shape=outs,
        in_specs=specs,
        out_specs=jax.tree.map(lambda _: VMEM, outs),
        scratch_shapes=scratch,
        compiler_params=pltpu.CompilerParams(vmem_limit_bytes=limit),
        cost_estimate=pl.CostEstimate(flops=flops, bytes_accessed=moved, transcendentals=0),
    )(*args)


def far(x):
    return pltpu.with_memory_space_constraint(x, pltpu.HBM)


def shape(dims, dtype):
    return jax.ShapeDtypeStruct(dims, dtype)


def sublane(block):
    return lax.broadcasted_iota(jnp.int32, block, 0)


def spread(rows, block):
    out = jnp.zeros(block, F32)
    for i, row in rows.items():
        out = jnp.where(sublane(block) == i, jnp.broadcast_to(row, block), out)
    return out


def part(pre_ref, dec_ref, index):
    quarter = pre_ref.shape[1] // 4
    start = pl.multiple_of(index * quarter, 128)
    return pre_ref[:, pl.ds(start, quarter)].astype(F32), dec_ref[:, pl.ds(start, quarter)].astype(F32)


def near(other=False):
    core = lax.axis_index("vocab") & 1
    return 2 - core if other else 1 + core


def pack(pre, dec, out_ref, at):
    half = pre.shape[1] // 2
    width = half + dec_width(pre.shape[1])
    out_ref[:, at : at + half] = jnp.concatenate([pre[:, :half], pre[:, half:]], axis=0).astype(BF16)
    out_ref[:, at + half : at + width] = fold(dec).astype(BF16)


def unpack(block, quarter):
    half = quarter // 2
    pre = block[:, :half].astype(F32)
    return jnp.concatenate([pre[:4], pre[4:]], axis=1), unfold(block[:, half:].astype(F32), quarter)


def load_kernel(pre_hbm, dec_hbm, pt_hbm, pre_ref, dec_ref, cross_ref, diag_ref, ids_ref, pt_ref, sems):
    pairs = ((pre_hbm, pre_ref), (dec_hbm, dec_ref), (pt_hbm, pt_ref))
    copies = [pltpu.make_async_copy(src, dst, sems.at[i]) for i, (src, dst) in enumerate(pairs)]
    for c in copies:
        c.start()
    for c in copies:
        c.wait()
    me = lax.axis_index("dp")
    pack(*part(pre_ref, dec_ref, me ^ near(other=True)), cross_ref, 0)
    pack(*part(pre_ref, dec_ref, me ^ 3), diag_ref, 0)
    ids = jnp.zeros(ids_ref.shape, jnp.int32)
    for i in range(pre_ref.shape[0]):
        ids = jnp.where(sublane(ids.shape) == i, pt_ref[i], ids)
    ids_ref[...] = ids


def digits_kernel(pre, ids_ref, dt_ref, out_ref):
    ids = jnp.where(sublane(ids_ref.shape) == pre, dt_ref[0], ids_ref[...])
    lane = lax.broadcasted_iota(jnp.int32, ids.shape, 1)
    low, mid, high = ids & (BASE - 1), (ids >> 7) & (BASE - 1), ids >> 14
    out_ref[...] = jnp.where(lane == 0, low, jnp.where(lane == 1, mid, high)).astype(F32).astype(BF16)


def join_kernel(pre_ref, dec_ref, cross_ref, out_ref):
    pack(*part(pre_ref, dec_ref, lax.axis_index("dp") ^ near()), out_ref, 0)
    width = cross_ref.shape[1]
    out_ref[:, width:] = cross_ref[...]


def dec_width(quarter):
    return -(-quarter // 1024) * 128


def fold(row):
    each = -(-row.shape[1] // 1024) * 128
    rows = {}
    for i in range(8):
        low, high = min(i * each, row.shape[1]), min((i + 1) * each, row.shape[1])
        if high > low:
            rows[i] = row[:, low:high]
            if high - low < each:
                rows[i] = jnp.concatenate([rows[i], jnp.zeros((1, each - high + low), row.dtype)], axis=1)
    return spread(rows, (8, each))


def unfold(block, width):
    return jnp.concatenate([block[i : i + 1] for i in range(8)], axis=1)[:, :width]


def dense_kernel(pre_ref, dec_ref, near_ref, diag_ref, ids_ref, out_ref):
    sets = [part(pre_ref, dec_ref, lax.axis_index("dp"))]
    quarter = sets[0][0].shape[1]
    half = quarter // 2
    width = diag_ref.shape[1]
    for block in (near_ref[:, :width], near_ref[:, width:], diag_ref[...]):
        sets.append(unpack(block, quarter))
    for pair in range(2):
        both = jnp.concatenate([sets[2 * pair][0], sets[2 * pair + 1][0]], axis=0)
        out_ref[:, pair * quarter : (pair + 1) * quarter] = both.astype(BF16)
    rows = {k + 4 * h: s[1][:, h * half : (h + 1) * half] for k, s in enumerate(sets) for h in range(2)}
    out_ref[:, 2 * quarter : 2 * quarter + half] = spread(rows, (8, half)).astype(BF16)
    out_ref[:, 2 * quarter + half :] = ids_ref[...]


def fetch_kernel(parts, head_hbm, out_ref, sems):
    rows = out_ref.shape[0]
    step = -(-(rows // parts) // 8) * 8
    copies = []
    for i in range(parts):
        block = pl.ds(i * step, min((i + 1) * step, rows) - i * step)
        copies.append(pltpu.make_async_copy(head_hbm.at[block], out_ref.at[block], sems.at[i]))
    for c in copies:
        c.start()
    for c in copies:
        c.wait()


def tiles_of(voc):
    wide = -(-voc // 128) * 128
    step = wide // TILES
    return [(t * step, min((t + 1) * step, voc)) for t in range(TILES)]


def encode(tile, t, powers, out_ref, rows, last_ref):
    most = jnp.maximum(jnp.max(jnp.abs(tile), axis=1, keepdims=True), TINY)
    powers.append(jnp.ceil(jnp.log2(most * (1.0 / MOST))))
    code = jnp.round(tile * jnp.exp2(-powers[-1]))
    count, width = tile.shape
    step = out_ref[0].shape[1] // TILES
    if t == TILES - 1:
        last_ref[:count, :width] = code
        for i, p in enumerate(powers):
            last_ref[:count, width + i : width + i + 1] = p
        code = last_ref[:count]
    code = code.astype(jnp.int32)
    for i, ref in enumerate(out_ref):
        ref[:, t * step : (t + 1) * step] = code[i * rows : (i + 1) * rows].astype(WIRE)


def decode(ref, t, low, high, voc):
    power = ref[:, voc + t : voc + t + 1].astype(F32)
    return ref[:, low:high].astype(F32) * jnp.exp2(power)


def matmul_kernel(n_dp, pre, voc, origins, head_ref, *refs):
    n_kv = len(origins)
    bufs, refs = refs[:n_kv], refs[n_kv:]
    own_ref, outs, (tgt_ref, x_ref, last_ref) = refs[0], refs[1:n_dp], refs[n_dp:]
    quarter = head_ref.shape[1]
    half = quarter // 2
    pre_rows = pre * n_kv
    rows = pre_rows + n_kv
    for buf, (crossed, z) in zip(bufs, origins):
        blocks = [buf[:, i * quarter : (i + 1) * quarter].astype(F32) for i in range(2)]
        decs = buf[:, 2 * quarter : 2 * quarter + half].astype(F32)
        for place in range(n_dp):
            base = rows * (0, 1 + crossed, 1 + crossed, 3)[place]
            kv = n_kv // 2 * (crossed ^ (place % 2)) + z
            low = pre * (place % 2)
            x_ref[base + pre * kv : base + pre * (kv + 1), :] = blocks[place // 2][low : low + pre]
            row = base + pre_rows + kv
            x_ref[row : row + 1, :half] = decs[place : place + 1]
            x_ref[row : row + 1, half:] = decs[n_dp + place : n_dp + place + 1]
        kv = n_kv // 2 * crossed + z
        digits = buf[:, 2 * quarter + half :].astype(F32)
        tgt_ref[pre * kv : pre * (kv + 1), :] = digits[:pre]
        tgt_ref[pre_rows + kv : pre_rows + kv + 1, :] = digits[pre : pre + 1]
    x = x_ref[...].astype(BF16)
    powers = []
    for t, (low, high) in enumerate(tiles_of(voc)):
        y = lax.dot_general(x, head_ref[low:high, :], (((1,), (1,)), ((), ())), preferred_element_type=F32)
        own_ref[:, low:high] = y[:rows]
        encode(y[rows:], t, powers, outs, rows, last_ref)


def stats_kernel(pre, n_kv, own_ref, p1, p2, p3, tgt_ref, out_ref, tile_ref):
    tile_ref[...] = jnp.zeros_like(tile_ref)
    rows, voc = own_ref.shape
    pre_rows = pre * n_kv
    parts = []
    for t, (low, high) in enumerate(tiles_of(voc)):
        total = own_ref[:, low:high]
        for p in (p1, p2, p3):
            total = total + decode(p, t, low, high, voc)
        parts.append(total)
    s = jnp.concatenate(parts, axis=1)
    digits = tgt_ref[...]
    ids = digits[:, 0:1] + BASE * digits[:, 1:2] + (BASE * BASE) * digits[:, 2:3]
    local = ids.astype(jnp.int32) - lax.axis_index("vocab") * voc
    columns = lax.broadcasted_iota(jnp.int32, s.shape, 1)
    top = jnp.max(s, axis=1, keepdims=True)
    total = jnp.sum(jnp.exp(s - top), axis=1, keepdims=True)
    picked = jnp.sum(jnp.where(columns == local, s, 0.0), axis=1, keepdims=True)
    lane = lax.broadcasted_iota(jnp.int32, (rows, 128), 1)
    st = jnp.where(lane == 0, top, jnp.where(lane == 1, total, picked))
    for kv in range(n_kv):
        tile_ref[BLOCK * kv : BLOCK * kv + pre, :] = st[pre * kv : pre * (kv + 1)]
        tile_ref[BLOCK * kv + pre : BLOCK * kv + pre + 1, :] = st[pre_rows + kv : pre_rows + kv + 1]
    out_ref[...] = jnp.transpose(tile_ref[...])[:8, :]


def merge(a, b):
    top = jnp.maximum(a[0:1], b[0:1])
    total = a[1:2] * jnp.exp(a[0:1] - top) + b[1:2] * jnp.exp(b[0:1] - top)
    return jnp.concatenate([top, total, a[2:3] + b[2:3]], axis=0)


def pair_kernel(mine_ref, other_ref, out_ref):
    other = pltpu.roll(other_ref[...], 64, 1)
    out_ref[0:3, :] = merge(mine_ref[...], other)
    out_ref[3:8, :] = jnp.zeros((5, 128), F32)


def final_kernel(pre, dec, mine_ref, r1, r2, r3, live_ref, pre_ref, dec_ref):
    total = mine_ref[...]
    for k, r in enumerate((r1, r2, r3), start=1):
        total = merge(total, pltpu.roll(r[...], 64 - BLOCK * k, 1))
    value = total[2:3] - (total[0:1] + jnp.log(total[1:2]))
    position = lax.axis_index("vocab") * dec
    pre_ref[...] = value[0, :pre]
    dec_ref[...] = jnp.where(position < live_ref[0], value[0, pre : pre + dec], 0.0)


def fast_body(n_dp, n_vocab, pre_hidden, dec_hidden, lm_head, pre_targets, dec_targets, dec_live):
    pre, dec = pre_hidden.shape[0], dec_hidden.shape[0]
    quarter, voc = lm_head.shape
    half = quarter // 2

    def swap(x, steps):
        pairs = []
        for d in range(n_dp):
            for v in range(n_vocab):
                kd, kv = steps(v)
                pairs.append((d * n_vocab + v, (d ^ kd) * n_vocab + (v ^ kv)))
        return lax.ppermute(x, ("dp", "vocab"), pairs)

    def core(v):
        return 0, 1

    def near_chip(v):
        return 1 + v % 2, 1

    def far_chip(v):
        return 3, 1

    def along(k, crossing):
        return lambda v: (0, 2 * k + crossing)

    def near_a(v):
        return 2 - v % 2, 0

    def near_b(v):
        return 1 + v % 2, 0

    def diagonal(v):
        return 3, 0

    narrow = half + dec_width(quarter)
    wide = -(-voc // 128) * 128
    pre_v, dec_v, cross, diag, ids = call(
        load_kernel,
        [shape(pre_hidden.shape, BF16), shape(dec_hidden.shape, BF16)]
        + [shape((8, narrow), BF16)] * 2
        + [shape((8, BASE), jnp.int32)],
        *map(far, (pre_hidden, dec_hidden, pre_targets)),
        specs=[HBM] * 3,
        scratch=[pltpu.SMEM(pre_targets.shape, jnp.int32), pltpu.SemaphoreType.DMA((3,))],
    )
    ids = call(
        functools.partial(digits_kernel, pre), shape((8, BASE), BF16), ids, dec_targets, specs=[VMEM, SMEM]
    )
    cross = swap(cross, core)
    diag = swap(diag, far_chip)
    joined = call(join_kernel, shape((8, 2 * narrow), BF16), pre_v, dec_v, cross, specs=[VMEM] * 3)
    joined = swap(joined, near_chip)
    head = call(
        functools.partial(fetch_kernel, 8),
        shape((voc, quarter), BF16),
        far(lm_head.T),
        specs=[HBM],
        scratch=[pltpu.SemaphoreType.DMA((8,))],
        moved=4 * quarter * voc,
    )
    mine = call(
        dense_kernel,
        shape((8, 2 * quarter + half + BASE), BF16),
        pre_v,
        dec_v,
        joined,
        diag,
        ids,
        specs=[VMEM] * 5,
    )
    chips = [mine] + [swap(mine, along(k, ROWS_CROSS)) for k in (1, 2, 3)]
    bufs = chips + [swap(b, core) for b in chips]
    origins = [(0, 0)] + [(ROWS_CROSS, k) for k in (1, 2, 3)] + [(1, 0)] + [(1 - ROWS_CROSS, k) for k in (1, 2, 3)]
    group = n_vocab * (pre + dec)
    rows = n_dp * group
    own, *parts, tgt = call(
        functools.partial(matmul_kernel, n_dp, pre, voc, origins),
        [shape((group, voc), F32)] + [shape((group, wide), WIRE)] * (n_dp - 1) + [shape((group, BASE), F32)],
        head,
        *bufs,
        specs=[VMEM] * (1 + n_vocab),
        scratch=[pltpu.VMEM((rows, quarter), F32), pltpu.VMEM((rows - group, wide // TILES), F32)],
        limit=16 << 20,
        flops=2 * rows * quarter * voc,
    )
    parts = [swap(p, f) for p, f in zip(parts, (near_a, near_b, diagonal))]
    stats = call(
        functools.partial(stats_kernel, pre, n_vocab),
        shape((8, 128), F32),
        own,
        *parts,
        tgt,
        specs=[VMEM] * 5,
        scratch=[pltpu.VMEM((128, 128), F32)],
    )
    both = call(pair_kernel, shape((8, 128), F32), stats, swap(stats, core), specs=[VMEM] * 2)
    others = [swap(both, along(k, 1)) for k in (1, 2, 3)]
    return tuple(
        call(
            functools.partial(final_kernel, pre, dec),
            [shape((pre,), F32), shape((dec,), F32)],
            both,
            *others,
            dec_live,
            specs=[VMEM] * 4 + [SMEM],
        )
    )


def plain_body(pre_hidden, dec_hidden, lm_head, pre_targets, dec_targets, dec_live):
    pre, dec = pre_hidden.shape[0], dec_hidden.shape[0]
    own = pre + dec
    voc = lm_head.shape[1]
    hidden = jnp.concatenate([pre_hidden, dec_hidden], axis=0)
    targets = jnp.concatenate([pre_targets, dec_targets], axis=0)
    me = lax.axis_index("vocab")
    group_hidden = lax.all_gather(hidden, "vocab", axis=0, tiled=True)
    group_targets = lax.all_gather(targets, "vocab", axis=0, tiled=True)
    every = lax.all_to_all(group_hidden, "dp", split_axis=1, concat_axis=0, tiled=True)
    partial = jnp.dot(every, lm_head, preferred_element_type=F32)
    logits = lax.psum_scatter(partial, "dp", scatter_dimension=0, tiled=True)
    hit = (group_targets - me * voc)[:, None] == jnp.arange(voc, dtype=jnp.int32)[None, :]
    picked = jnp.sum(jnp.where(hit, logits, 0.0), axis=1)
    top = lax.pmax(jnp.max(logits, axis=1), "vocab")
    total = jnp.sum(jnp.exp(logits - top[:, None]), axis=1)
    total, picked = lax.psum((total, picked), "vocab")
    values = lax.dynamic_slice_in_dim(picked - (top + jnp.log(total)), me * own, own, 0)
    positions = me * dec + jnp.arange(dec, dtype=jnp.int32)
    return values[:pre], jnp.where(positions < dec_live[0], values[pre:], 0.0)


def solution(mesh):
    n_dp, n_vocab = mesh.shape["dp"], mesh.shape["vocab"]

    def body(pre_hidden, dec_hidden, lm_head, *rest):
        quarter, voc = lm_head.shape
        fits = (n_dp, n_vocab, pre_hidden.shape[0], dec_hidden.shape[0]) == (4, 8, 4, 1)
        fits = fits and quarter % 256 == 0 and TILES <= -voc % 128 and -(-voc // 128) % TILES == 0
        run = functools.partial(fast_body, n_dp, n_vocab) if fits else plain_body
        return run(pre_hidden, dec_hidden, lm_head, *rest)

    rows = P(("dp", "vocab"))
    in_specs = (P(("dp", "vocab"), None), P(("dp", "vocab"), None), P("dp", "vocab"), rows, rows, P("dp"))
    return jax.shard_map(body, mesh=mesh, in_specs=in_specs, out_specs=(rows, rows), check_vma=False)
```

time: 45.4 us -> 47.1 us (1.037)
  starting transfers between devices: 17.5 us -> 19.1 us
  waiting for transfers between devices: 16.4 us -> 17.8 us
  local copies, waits for them, and re-layouts: 0.65 us -> 0 us
  Pallas kernels: 8.49 us -> 8 us
    ppermute x17, starting transfers between devices: 17.5 us -> 19.1 us  [swap(): return lax.ppermute(x, ('dp', 'vocab'), pairs)]
    ppermute x17, waiting for transfers between devices: 16.4 us -> 17.8 us  [swap(): return lax.ppermute(x, ('dp', 'vocab'), pairs)]
    unnamed x2 -> x0, local copies, waits for them, and re-layouts: 0.65 us -> none
    pallas_call x8 -> x9, Pallas kernels: 8.49 us -> 8 us  [call(): pl.pallas_call(kernel, out_shape=outs, in_specs=specs, out_specs=jax.tree...]
  transfers between devices with their start and end apart: 17 -> 17, of which waited for: 8 -> 9; matrix products, arithmetic and copies ran while one was open for 0% -> 0% of each run, Pallas kernels for 8% -> 7%
where the time goes in v2:
time: 47.1 us; the launch traced here: 46.9 us
  starting transfers between devices  19.1 us (41%)
  waiting for transfers between devices  17.8 us (38%)
  Pallas kernels  8 us (17%)
  between operations  2.03 us (4%)
    ppermute x17, starting transfers between devices, swap(): return lax.ppermute(x, ('dp', 'vocab'), pairs)  19.1 us
    ppermute x17, waiting for transfers between devices, swap(): return lax.ppermute(x, ('dp', 'vocab'), pairs)  17.8 us
    pallas_call x9, Pallas kernels, call(): pl.pallas_call(kernel, out_shape=outs, in_specs=specs, out_specs=jax.tree...  8 us
  transfers between devices with their start and end apart: 17, of which 9 were waited for; matrix products, arithmetic and copies ran while one was open for 0% of the time, Pallas kernels for 7%

profile of v2, /device:TPU:0, one launch (start us, length us, event | category | flops | bytes accessed | tf_op | source)
XLA Modules:
  0.0 46.9 jit_solution(13241408865674993305)
XLA Ops:
  0.6 0.9 %shard_map.78 = (bf16[4,7168]{1,0:T(4,128)(2,1)S(1)}, bf16[1,7168]{1,0:T(2,128)(2,1)S(1)}, bf16[8,1152]{1,0:T(8,128)(2,1)S(1)}, bf16[8,1152]{1,0:T(8,128)(2,1)S(1)}, s32[8,128]{1,0:T(8,128)S(1)}) custom-call(bf16[4,7168]{1,0:T(4,128)(2,1)} %pre_hbm.1, bf16[1,7168]{1,0:T(2,128)(2,1)} %dec_hbm.1, s32[4]{0:T(128)} %pt_hbm.1), custom_call_target="tpu_custom_call" | custom-call | tf_op jit(solution)/shard_map/pallas_call | solution.py:25
  1.5 0.6 %collective-permute-start = (bf16[8,1152]{1,0:T(8,128)(2,1)S(1)}, bf16[8,1152]{1,0:T(8,128)(2,1)S(1)}, u32[]{:S(2)}, u32[]{:S(2)}) collective-permute-start(bf16[8,1152]{1,0:T(8,128)(2,1)S(1)} %get-tuple-element.14), channel_id=1, source_target_pairs={{0,1},{1,0},{2,3},{3,2},{4,5},{5,4},{6,7},{7,6},{8,9},{9,8},{10,11... | collective-permute-start | bytes 55304 | tf_op jit(solution)/shard_map/ppermute | solution.py:273
  2.1 0.8 %collective-permute-done.cross_ref = bf16[8,1152]{1,0:T(8,128)(2,1)S(1)} collective-permute-done((bf16[8,1152]{1,0:T(8,128)(2,1)S(1)}, bf16[8,1152]{1,0:T(8,128)(2,1)S(1)}, u32[]{:S(2)}, u32[]{:S(2)}) %collective-permute-start) | collective-permute-done | bytes 18464 | tf_op jit(solution)/shard_map/ppermute | solution.py:273
  2.9 2.6 %collective-permute-start.1 = (bf16[8,2304]{1,0:T(8,128)(2,1)S(1)}, bf16[8,2304]{1,0:T(8,128)(2,1)S(1)}, u32[]{:S(2)}, u32[]{:S(2)}) collective-permute-start(bf16[8,2304]{1,0:T(8,128)(2,1)S(1)} %shard_map.79), channel_id=1, source_target_pairs={{0,9},{1,16},{2,11},{3,18},{4,13},{5,20},{6,15},{7,22},{8,1},{9,24... | collective-permute-start | bytes 110600 | tf_op jit(solution)/shard_map/ppermute | solution.py:273
  5.6 1.4 %collective-permute-start.2 = (bf16[8,1152]{1,0:T(8,128)(2,1)S(1)}, bf16[8,1152]{1,0:T(8,128)(2,1)S(1)}, u32[]{:S(2)}, u32[]{:S(2)}) collective-permute-start(bf16[8,1152]{1,0:T(8,128)(2,1)S(1)} %get-tuple-element.15), channel_id=1, source_target_pairs={{0,25},{1,24},{2,27},{3,26},{4,29},{5,28},{6,31},{7,30},{8,17},{9,... | collective-permute-start | bytes 55304 | tf_op jit(solution)/shard_map/ppermute | solution.py:273
  7.7 2.0 %collective-permute-done.2.diag_ref = bf16[8,1152]{1,0:T(8,128)(2,1)S(1)} collective-permute-done((bf16[8,1152]{1,0:T(8,128)(2,1)S(1)}, bf16[8,1152]{1,0:T(8,128)(2,1)S(1)}, u32[]{:S(2)}, u32[]{:S(2)}) %collective-permute-start.2) | collective-permute-done | bytes 18464 | tf_op jit(solution)/shard_map/ppermute | solution.py:273
  9.7 0.0 collective-permute-done.1.near_ref
  9.7 1.6 %collective-permute-start.3 = (bf16[8,4608]{1,0:T(8,128)(2,1)S(1)}, bf16[8,4608]{1,0:T(8,128)(2,1)S(1)}, u32[]{:S(2)}, u32[]{:S(2)}) collective-permute-start(bf16[8,4608]{1,0:T(8,128)(2,1)S(1)} %shard_map.81.refs_0_), channel_id=1, source_target_pairs={{0,3},{1,2},{2,1},{3,0},{4,7},{5,6},{6,5},{7,4},{8,11},{9,10},{10,... | collective-permute-start | bytes 221192 | tf_op jit(solution)/shard_map/ppermute | solution.py:273
  11.4 2.3 %collective-permute-start.4 = (bf16[8,4608]{1,0:T(8,128)(2,1)S(1)}, bf16[8,4608]{1,0:T(8,128)(2,1)S(1)}, u32[]{:S(2)}, u32[]{:S(2)}) collective-permute-start(bf16[8,4608]{1,0:T(8,128)(2,1)S(1)} %shard_map.81.refs_0_), channel_id=1, source_target_pairs={{0,5},{1,4},{2,7},{3,6},{4,1},{5,0},{6,3},{7,2},{8,13},{9,12},{10,... | collective-permute-start | bytes 221192 | tf_op jit(solution)/shard_map/ppermute | solution.py:273
  13.7 0.2 collective-permute-start.5
  13.9 0.2 collective-permute-start.6
  14.1 0.0 collective-permute-done.3.refs_1_
  14.1 0.3 collective-permute-start.7
  14.4 3.7 %collective-permute-done.4.refs_2_ = bf16[8,4608]{1,0:T(8,128)(2,1)S(1)} collective-permute-done((bf16[8,4608]{1,0:T(8,128)(2,1)S(1)}, bf16[8,4608]{1,0:T(8,128)(2,1)S(1)}, u32[]{:S(2)}, u32[]{:S(2)}) %collective-permute-start.4) | collective-permute-done | bytes 73760 | tf_op jit(solution)/shard_map/ppermute | solution.py:273
  18.1 2.0 %collective-permute-start.8 = (bf16[8,4608]{1,0:T(8,128)(2,1)S(1)}, bf16[8,4608]{1,0:T(8,128)(2,1)S(1)}, u32[]{:S(2)}, u32[]{:S(2)}) collective-permute-start(bf16[8,4608]{1,0:T(8,128)(2,1)S(1)} %collective-permute-done.4.refs_2_), channel_id=1, source_target_pairs={{0,1},{1,0},{2,3},{3,2},{4,5},{5,4},{6,7},{7,6},{8,9},{9,8},{10,11... | collective-permute-start | bytes 221192 | tf_op jit(solution)/shard_map/ppermute | solution.py:273
  20.1 0.0 collective-permute-done.5.refs_3_
  20.1 0.0 collective-permute-start.9
  20.1 3.1 %shard_map.77.head_ref = bf16[2020,1792]{1,0:T(8,128)(2,1)S(1)} custom-call(bf16[2020,1792]{1,0:T(8,128)(2,1)} %bitcast.1), custom_call_target="tpu_custom_call" | custom-call | bytes 14479360 | tf_op jit(solution)/shard_map/pallas_call | solution.py:25
  23.3 0.0 collective-permute-done.6.refs_4_
  23.3 0.0 collective-permute-done.7.refs_5_
  23.3 0.0 collective-permute-done.8.refs_6_
  23.3 0.0 collective-permute-done.9.refs_7_
  23.3 2.7 %shard_map.82 = (f32[40,2020]{1,0:T(8,128)S(1)}, s16[40,2048]{1,0:T(8,128)(2,1)S(1)}, s16[40,2048]{1,0:T(8,128)(2,1)S(1)}, s16[40,2048]{1,0:T(8,128)(2,1)S(1)}, f32[40,128]{1,0:T(8,128)S(1)}) custom-call(bf16[2020,1792]{1,0:T(8,128)(2,1)S(1)} %shard_map.77.head_ref, bf16[8,4608]{1,0:T(8,128)(2,1)S(1)} %shard_map.81.refs_0_, ...), custom_call_target="tpu_custom_call" | custom-call | flops 1158348800 | tf_op jit(solution)/shard_map/pallas_call | solution.py:25
  26.0 1.2 %collective-permute-start.10 = (s16[40,2048]{1,0:T(8,128)(2,1)S(1)}, s16[40,2048]{1,0:T(8,128)(2,1)S(1)}, u32[]{:S(2)}, u32[]{:S(2)}) collective-permute-start(s16[40,2048]{1,0:T(8,128)(2,1)S(1)} %get-tuple-element.18), channel_id=1, source_target_pairs={{0,16},{1,9},{2,18},{3,11},{4,20},{5,13},{6,22},{7,15},{8,24},{9,1... | collective-permute-start | bytes 491528 | tf_op jit(solution)/shard_map/ppermute | solution.py:273
  27.2 0.9 %collective-permute-start.11 = (s16[40,2048]{1,0:T(8,128)(2,1)S(1)}, s16[40,2048]{1,0:T(8,128)(2,1)S(1)}, u32[]{:S(2)}, u32[]{:S(2)}) collective-permute-start(s16[40,2048]{1,0:T(8,128)(2,1)S(1)} %get-tuple-element.19), channel_id=1, source_target_pairs={{0,8},{1,17},{2,10},{3,19},{4,12},{5,21},{6,14},{7,23},{8,0},{9,25... | collective-permute-start | bytes 491528 | tf_op jit(solution)/shard_map/ppermute | solution.py:273
  28.1 1.4 %collective-permute-start.12 = (s16[40,2048]{1,0:T(8,128)(2,1)S(1)}, s16[40,2048]{1,0:T(8,128)(2,1)S(1)}, u32[]{:S(2)}, u32[]{:S(2)}) collective-permute-start(s16[40,2048]{1,0:T(8,128)(2,1)S(1)} %get-tuple-element.20), channel_id=1, source_target_pairs={{0,24},{1,25},{2,26},{3,27},{4,28},{5,29},{6,30},{7,31},{8,16},{9,... | collective-permute-start | bytes 491528 | tf_op jit(solution)/shard_map/ppermute | solution.py:273
  29.6 3.5 %collective-permute-done.10.p1 = s16[40,2048]{1,0:T(8,128)(2,1)S(1)} collective-permute-done((s16[40,2048]{1,0:T(8,128)(2,1)S(1)}, s16[40,2048]{1,0:T(8,128)(2,1)S(1)}, u32[]{:S(2)}, u32[]{:S(2)}) %collective-permute-start.10) | collective-permute-done | bytes 163872 | tf_op jit(solution)/shard_map/ppermute | solution.py:273
  33.1 0.8 %collective-permute-done.11.p2 = s16[40,2048]{1,0:T(8,128)(2,1)S(1)} collective-permute-done((s16[40,2048]{1,0:T(8,128)(2,1)S(1)}, s16[40,2048]{1,0:T(8,128)(2,1)S(1)}, u32[]{:S(2)}, u32[]{:S(2)}) %collective-permute-start.11) | collective-permute-done | bytes 163872 | tf_op jit(solution)/shard_map/ppermute | solution.py:273
  33.9 2.9 %collective-permute-done.12.p3 = s16[40,2048]{1,0:T(8,128)(2,1)S(1)} collective-permute-done((s16[40,2048]{1,0:T(8,128)(2,1)S(1)}, s16[40,2048]{1,0:T(8,128)(2,1)S(1)}, u32[]{:S(2)}, u32[]{:S(2)}) %collective-permute-start.12) | collective-permute-done | bytes 163872 | tf_op jit(solution)/shard_map/ppermute | solution.py:273
  36.7 0.4 shard_map.83.mine_ref
  37.2 0.0 collective-permute-start.13
  37.2 1.2 %collective-permute-done.13.other_ref = f32[8,128]{1,0:T(8,128)S(1)} collective-permute-done((f32[8,128]{1,0:T(8,128)S(1)}, f32[8,128]{1,0:T(8,128)S(1)}, u32[]{:S(2)}, u32[]{:S(2)}) %collective-permute-start.13) | collective-permute-done | bytes 4128 | tf_op jit(solution)/shard_map/ppermute | solution.py:273
  38.4 0.1 shard_map.84.mine_ref
  38.5 1.8 %collective-permute-start.14 = (f32[8,128]{1,0:T(8,128)S(1)}, f32[8,128]{1,0:T(8,128)S(1)}, u32[]{:S(2)}, u32[]{:S(2)}) collective-permute-start(f32[8,128]{1,0:T(8,128)S(1)} %shard_map.84.mine_ref), channel_id=1, source_target_pairs={{0,3},{1,2},{2,1},{3,0},{4,7},{5,6},{6,5},{7,4},{8,11},{9,10},{10,... | collective-permute-start | bytes 12296 | tf_op jit(solution)/shard_map/ppermute | solution.py:273
  40.3 1.2 %collective-permute-start.15 = (f32[8,128]{1,0:T(8,128)S(1)}, f32[8,128]{1,0:T(8,128)S(1)}, u32[]{:S(2)}, u32[]{:S(2)}) collective-permute-start(f32[8,128]{1,0:T(8,128)S(1)} %shard_map.84.mine_ref), channel_id=1, source_target_pairs={{0,5},{1,4},{2,7},{3,6},{4,1},{5,0},{6,3},{7,2},{8,13},{9,12},{10,... | collective-permute-start | bytes 12296 | tf_op jit(solution)/shard_map/ppermute | solution.py:273
  41.4 1.2 %collective-permute-start.16 = (f32[8,128]{1,0:T(8,128)S(1)}, f32[8,128]{1,0:T(8,128)S(1)}, u32[]{:S(2)}, u32[]{:S(2)}) collective-permute-start(f32[8,128]{1,0:T(8,128)S(1)} %shard_map.84.mine_ref), channel_id=1, source_target_pairs={{0,7},{1,6},{2,5},{3,4},{4,3},{5,2},{6,1},{7,0},{8,15},{9,14},{10,... | collective-permute-start | bytes 12296 | tf_op jit(solution)/shard_map/ppermute | solution.py:273
  43.3 0.0 collective-permute-done.14.r1
  43.3 0.9 %collective-permute-done.15.r2 = f32[8,128]{1,0:T(8,128)S(1)} collective-permute-done((f32[8,128]{1,0:T(8,128)S(1)}, f32[8,128]{1,0:T(8,128)S(1)}, u32[]{:S(2)}, u32[]{:S(2)}) %collective-permute-start.15) | collective-permute-done | bytes 4128 | tf_op jit(solution)/shard_map/ppermute | solution.py:273
  44.2 2.1 %collective-permute-done.16.r3 = f32[8,128]{1,0:T(8,128)S(1)} collective-permute-done((f32[8,128]{1,0:T(8,128)S(1)}, f32[8,128]{1,0:T(8,128)S(1)}, u32[]{:S(2)}, u32[]{:S(2)}) %collective-permute-start.16) | collective-permute-done | bytes 4128 | tf_op jit(solution)/shard_map/ppermute | solution.py:273
  46.2 0.7 %shard_map.85 = (f32[4]{0:T(128)}, f32[1]{0:T(128)}) custom-call(f32[8,128]{1,0:T(8,128)S(1)} %shard_map.84.mine_ref, f32[8,128]{1,0:T(8,128)S(1)} %collective-permute-done.14.r1, f32[8,128]{1,0:T(8,128)S(1)} %collective-permute-done.15.r2, f32[8,128]{1,0:T(8,128)S(1)} %collective-permute-done.16.r3, s32[1]{0:T(128)S(6)} %copy.9.live_ref), custom_call_target="tpu_custom_call" | custom-call | tf_op jit(solution)/shard_map/pallas_call | solution.py:25
  (3 shorter events, 0.1 us)
Async XLA Ops:
  1.5 1.4 %collective-permute-start = (bf16[8,1152]{1,0:T(8,128)(2,1)S(1)}, bf16[8,1152]{1,0:T(8,128)(2,1)S(1)}, u32[]{:S(2)}, u32[]{:S(2)}) collective-permute-start(bf16[8,1152]{1,0:T(8,128)(2,1)S(1)} %get-tuple-element.14), channel_id=1, source_target_pairs={{0,1},{1,0},{2,3},{3,2},{4,5},{5,4},{6,7},{7,6},{8,9},{9,8},{10,11... | collective-permute-start | bytes 55304 | tf_op jit(solution)/shard_map/ppermute | solution.py:273
  2.9 6.7 %collective-permute-start.1 = (bf16[8,2304]{1,0:T(8,128)(2,1)S(1)}, bf16[8,2304]{1,0:T(8,128)(2,1)S(1)}, u32[]{:S(2)}, u32[]{:S(2)}) collective-permute-start(bf16[8,2304]{1,0:T(8,128)(2,1)S(1)} %shard_map.79), channel_id=1, source_target_pairs={{0,9},{1,16},{2,11},{3,18},{4,13},{5,20},{6,15},{7,22},{8,1},{9,24... | collective-permute-start | bytes 110600 | tf_op jit(solution)/shard_map/ppermute | solution.py:273
  5.6 4.1 %collective-permute-start.2 = (bf16[8,1152]{1,0:T(8,128)(2,1)S(1)}, bf16[8,1152]{1,0:T(8,128)(2,1)S(1)}, u32[]{:S(2)}, u32[]{:S(2)}) collective-permute-start(bf16[8,1152]{1,0:T(8,128)(2,1)S(1)} %get-tuple-element.15), channel_id=1, source_target_pairs={{0,25},{1,24},{2,27},{3,26},{4,29},{5,28},{6,31},{7,30},{8,17},{9,... | collective-permute-start | bytes 55304 | tf_op jit(solution)/shard_map/ppermute | solution.py:273
  9.7 4.3 %collective-permute-start.3 = (bf16[8,4608]{1,0:T(8,128)(2,1)S(1)}, bf16[8,4608]{1,0:T(8,128)(2,1)S(1)}, u32[]{:S(2)}, u32[]{:S(2)}) collective-permute-start(bf16[8,4608]{1,0:T(8,128)(2,1)S(1)} %shard_map.81.refs_0_), channel_id=1, source_target_pairs={{0,3},{1,2},{2,1},{3,0},{4,7},{5,6},{6,5},{7,4},{8,11},{9,10},{10,... | collective-permute-start | bytes 221192 | tf_op jit(solution)/shard_map/ppermute | solution.py:273
  11.4 6.7 %collective-permute-start.4 = (bf16[8,4608]{1,0:T(8,128)(2,1)S(1)}, bf16[8,4608]{1,0:T(8,128)(2,1)S(1)}, u32[]{:S(2)}, u32[]{:S(2)}) collective-permute-start(bf16[8,4608]{1,0:T(8,128)(2,1)S(1)} %shard_map.81.refs_0_), channel_id=1, source_target_pairs={{0,5},{1,4},{2,7},{3,6},{4,1},{5,0},{6,3},{7,2},{8,13},{9,12},{10,... | collective-permute-start | bytes 221192 | tf_op jit(solution)/shard_map/ppermute | solution.py:273
  13.7 6.4 %collective-permute-start.5 = (bf16[8,4608]{1,0:T(8,128)(2,1)S(1)}, bf16[8,4608]{1,0:T(8,128)(2,1)S(1)}, u32[]{:S(2)}, u32[]{:S(2)}) collective-permute-start(bf16[8,4608]{1,0:T(8,128)(2,1)S(1)} %shard_map.81.refs_0_), channel_id=1, source_target_pairs={{0,7},{1,6},{2,5},{3,4},{4,3},{5,2},{6,1},{7,0},{8,15},{9,14},{10,... | collective-permute-start | bytes 221192 | tf_op jit(solution)/shard_map/ppermute | solution.py:273
  13.9 9.4 %collective-permute-start.6 = (bf16[8,4608]{1,0:T(8,128)(2,1)S(1)}, bf16[8,4608]{1,0:T(8,128)(2,1)S(1)}, u32[]{:S(2)}, u32[]{:S(2)}) collective-permute-start(bf16[8,4608]{1,0:T(8,128)(2,1)S(1)} %shard_map.81.refs_0_), channel_id=1, source_target_pairs={{0,1},{1,0},{2,3},{3,2},{4,5},{5,4},{6,7},{7,6},{8,9},{9,8},{10,11... | collective-permute-start | bytes 221192 | tf_op jit(solution)/shard_map/ppermute | solution.py:273
  14.1 9.2 %collective-permute-start.7 = (bf16[8,4608]{1,0:T(8,128)(2,1)S(1)}, bf16[8,4608]{1,0:T(8,128)(2,1)S(1)}, u32[]{:S(2)}, u32[]{:S(2)}) collective-permute-start(bf16[8,4608]{1,0:T(8,128)(2,1)S(1)} %collective-permute-done.3.refs_1_), channel_id=1, source_target_pairs={{0,1},{1,0},{2,3},{3,2},{4,5},{5,4},{6,7},{7,6},{8,9},{9,8},{10,11... | collective-permute-start | bytes 221192 | tf_op jit(solution)/shard_map/ppermute | solution.py:273
  18.1 5.2 %collective-permute-start.8 = (bf16[8,4608]{1,0:T(8,128)(2,1)S(1)}, bf16[8,4608]{1,0:T(8,128)(2,1)S(1)}, u32[]{:S(2)}, u32[]{:S(2)}) collective-permute-start(bf16[8,4608]{1,0:T(8,128)(2,1)S(1)} %collective-permute-done.4.refs_2_), channel_id=1, source_target_pairs={{0,1},{1,0},{2,3},{3,2},{4,5},{5,4},{6,7},{7,6},{8,9},{9,8},{10,11... | collective-permute-start | bytes 221192 | tf_op jit(solution)/shard_map/ppermute | solution.py:273
  20.1 3.2 %collective-permute-start.9 = (bf16[8,4608]{1,0:T(8,128)(2,1)S(1)}, bf16[8,4608]{1,0:T(8,128)(2,1)S(1)}, u32[]{:S(2)}, u32[]{:S(2)}) collective-permute-start(bf16[8,4608]{1,0:T(8,128)(2,1)S(1)} %collective-permute-done.5.refs_3_), channel_id=1, source_target_pairs={{0,1},{1,0},{2,3},{3,2},{4,5},{5,4},{6,7},{7,6},{8,9},{9,8},{10,11... | collective-permute-start | bytes 221192 | tf_op jit(solution)/shard_map/ppermute | solution.py:273
  26.0 7.1 %collective-permute-start.10 = (s16[40,2048]{1,0:T(8,128)(2,1)S(1)}, s16[40,2048]{1,0:T(8,128)(2,1)S(1)}, u32[]{:S(2)}, u32[]{:S(2)}) collective-permute-start(s16[40,2048]{1,0:T(8,128)(2,1)S(1)} %get-tuple-element.18), channel_id=1, source_target_pairs={{0,16},{1,9},{2,18},{3,11},{4,20},{5,13},{6,22},{7,15},{8,24},{9,1... | collective-permute-start | bytes 491528 | tf_op jit(solution)/shard_map/ppermute | solution.py:273
  27.2 6.7 %collective-permute-start.11 = (s16[40,2048]{1,0:T(8,128)(2,1)S(1)}, s16[40,2048]{1,0:T(8,128)(2,1)S(1)}, u32[]{:S(2)}, u32[]{:S(2)}) collective-permute-start(s16[40,2048]{1,0:T(8,128)(2,1)S(1)} %get-tuple-element.19), channel_id=1, source_target_pairs={{0,8},{1,17},{2,10},{3,19},{4,12},{5,21},{6,14},{7,23},{8,0},{9,25... | collective-permute-start | bytes 491528 | tf_op jit(solution)/shard_map/ppermute | solution.py:273
  28.1 8.6 %collective-permute-start.12 = (s16[40,2048]{1,0:T(8,128)(2,1)S(1)}, s16[40,2048]{1,0:T(8,128)(2,1)S(1)}, u32[]{:S(2)}, u32[]{:S(2)}) collective-permute-start(s16[40,2048]{1,0:T(8,128)(2,1)S(1)} %get-tuple-element.20), channel_id=1, source_target_pairs={{0,24},{1,25},{2,26},{3,27},{4,28},{5,29},{6,30},{7,31},{8,16},{9,... | collective-permute-start | bytes 491528 | tf_op jit(solution)/shard_map/ppermute | solution.py:273
  37.2 1.2 %collective-permute-start.13 = (f32[8,128]{1,0:T(8,128)S(1)}, f32[8,128]{1,0:T(8,128)S(1)}, u32[]{:S(2)}, u32[]{:S(2)}) collective-permute-start(f32[8,128]{1,0:T(8,128)S(1)} %shard_map.83.mine_ref), channel_id=1, source_target_pairs={{0,1},{1,0},{2,3},{3,2},{4,5},{5,4},{6,7},{7,6},{8,9},{9,8},{10,11... | collective-permute-start | bytes 12296 | tf_op jit(solution)/shard_map/ppermute | solution.py:273
  38.5 4.8 %collective-permute-start.14 = (f32[8,128]{1,0:T(8,128)S(1)}, f32[8,128]{1,0:T(8,128)S(1)}, u32[]{:S(2)}, u32[]{:S(2)}) collective-permute-start(f32[8,128]{1,0:T(8,128)S(1)} %shard_map.84.mine_ref), channel_id=1, source_target_pairs={{0,3},{1,2},{2,1},{3,0},{4,7},{5,6},{6,5},{7,4},{8,11},{9,10},{10,... | collective-permute-start | bytes 12296 | tf_op jit(solution)/shard_map/ppermute | solution.py:273
  40.3 3.9 %collective-permute-start.15 = (f32[8,128]{1,0:T(8,128)S(1)}, f32[8,128]{1,0:T(8,128)S(1)}, u32[]{:S(2)}, u32[]{:S(2)}) collective-permute-start(f32[8,128]{1,0:T(8,128)S(1)} %shard_map.84.mine_ref), channel_id=1, source_target_pairs={{0,5},{1,4},{2,7},{3,6},{4,1},{5,0},{6,3},{7,2},{8,13},{9,12},{10,... | collective-permute-start | bytes 12296 | tf_op jit(solution)/shard_map/ppermute | solution.py:273
  41.4 4.8 %collective-permute-start.16 = (f32[8,128]{1,0:T(8,128)S(1)}, f32[8,128]{1,0:T(8,128)S(1)}, u32[]{:S(2)}, u32[]{:S(2)}) collective-permute-start(f32[8,128]{1,0:T(8,128)S(1)} %shard_map.84.mine_ref), channel_id=1, source_target_pairs={{0,7},{1,6},{2,5},{3,4},{4,3},{5,2},{6,1},{7,0},{8,15},{9,14},{10,... | collective-permute-start | bytes 12296 | tf_op jit(solution)/shard_map/ppermute | solution.py:273

commit v3 on v2

--- a/solution.py
+++ b/solution.py
@@ -21,13 +21,14 @@
 F32, BF16 = jnp.float32, jnp.bfloat16
 
 
-def call(kernel, outs, *args, specs, scratch=(), limit=8 << 20, flops=0, moved=0):
+def call(kernel, outs, *args, specs, out_specs=None, scratch=(), limit=8 << 20, flops=0, moved=0, aliases=None):
     return pl.pallas_call(
         kernel,
         out_shape=outs,
         in_specs=specs,
-        out_specs=jax.tree.map(lambda _: VMEM, outs),
+        out_specs=out_specs or jax.tree.map(lambda _: VMEM, outs),
         scratch_shapes=scratch,
+        input_output_aliases=aliases or {},
         compiler_params=pltpu.CompilerParams(vmem_limit_bytes=limit),
         cost_estimate=pl.CostEstimate(flops=flops, bytes_accessed=moved, transcendentals=0),
     )(*args)
@@ -77,7 +78,9 @@
 
 
 def load_kernel(pre_hbm, dec_hbm, pt_hbm, pre_ref, dec_ref, cross_ref, diag_ref, ids_ref, pt_ref, sems):
-    pairs = ((pre_hbm, pre_ref), (dec_hbm, dec_ref), (pt_hbm, pt_ref))
+    quarter = pre_ref.shape[1] // 4
+    cuts = [pl.ds(i * quarter, quarter) for i in range(4)]
+    pairs = [(pre_hbm.at[:, c], pre_ref.at[:, c]) for c in cuts] + [(dec_hbm, dec_ref), (pt_hbm, pt_ref)]
     copies = [pltpu.make_async_copy(src, dst, sems.at[i]) for i, (src, dst) in enumerate(pairs)]
     for c in copies:
         c.start()
@@ -180,33 +183,41 @@
     return ref[:, low:high].astype(F32) * jnp.exp2(power)
 
 
-def matmul_kernel(n_dp, pre, voc, origins, head_ref, *refs):
-    n_kv = len(origins)
-    bufs, refs = refs[:n_kv], refs[n_kv:]
-    own_ref, outs, (tgt_ref, x_ref, last_ref) = refs[0], refs[1:n_dp], refs[n_dp:]
-    quarter = head_ref.shape[1]
+def place_rows(n_kv, pre, bufs, origins, x_ref, tgt_ref):
+    rows, quarter = x_ref.shape[0] // 4, x_ref.shape[1]
     half = quarter // 2
     pre_rows = pre * n_kv
-    rows = pre_rows + n_kv
     for buf, (crossed, z) in zip(bufs, origins):
         blocks = [buf[:, i * quarter : (i + 1) * quarter].astype(F32) for i in range(2)]
         decs = buf[:, 2 * quarter : 2 * quarter + half].astype(F32)
-        for place in range(n_dp):
+        for place in range(4):
             base = rows * (0, 1 + crossed, 1 + crossed, 3)[place]
             kv = n_kv // 2 * (crossed ^ (place % 2)) + z
             low = pre * (place % 2)
             x_ref[base + pre * kv : base + pre * (kv + 1), :] = blocks[place // 2][low : low + pre]
             row = base + pre_rows + kv
             x_ref[row : row + 1, :half] = decs[place : place + 1]
-            x_ref[row : row + 1, half:] = decs[n_dp + place : n_dp + place + 1]
+            x_ref[row : row + 1, half:] = decs[4 + place : 4 + place + 1]
         kv = n_kv // 2 * crossed + z
         digits = buf[:, 2 * quarter + half :].astype(F32)
         tgt_ref[pre * kv : pre * (kv + 1), :] = digits[:pre]
         tgt_ref[pre_rows + kv : pre_rows + kv + 1, :] = digits[pre : pre + 1]
+
+
+def early_kernel(n_kv, pre, origins, *refs):
+    place_rows(n_kv, pre, refs[:-2], origins, *refs[-2:])
+
+
+def matmul_kernel(n_dp, n_kv, pre, voc, origins, head_ref, *refs):
+    bufs, refs = refs[: len(origins)], refs[len(origins) + 2 :]
+    own_ref, outs, (x_ref, tgt_ref, last_ref) = refs[0], refs[1:n_dp], refs[n_dp:]
+    rows = x_ref.shape[0] // n_dp
+    place_rows(n_kv, pre, bufs, origins, x_ref, tgt_ref)
     x = x_ref[...].astype(BF16)
     powers = []
     for t, (low, high) in enumerate(tiles_of(voc)):
-        y = lax.dot_general(x, head_ref[low:high, :], (((1,), (1,)), ((), ())), preferred_element_type=F32)
+        y = lax.dot_general(head_ref[low:high, :], x, (((1,), (1,)), ((), ())), preferred_element_type=F32)
+        y = jnp.transpose(y)
         own_ref[:, low:high] = y[:rows]
         encode(y[rows:], t, powers, outs, rows, last_ref)
 
@@ -249,7 +260,7 @@
     out_ref[3:8, :] = jnp.zeros((5, 128), F32)
 
 
-def final_kernel(pre, dec, mine_ref, r1, r2, r3, live_ref, pre_ref, dec_ref):
+def final_kernel(pre, dec, mine_ref, r1, r2, r3, live_ref, pre_hbm, dec_hbm, pre_ref, dec_ref, sems):
     total = mine_ref[...]
     for k, r in enumerate((r1, r2, r3), start=1):
         total = merge(total, pltpu.roll(r[...], 64 - BLOCK * k, 1))
@@ -257,6 +268,14 @@
     position = lax.axis_index("vocab") * dec
     pre_ref[...] = value[0, :pre]
     dec_ref[...] = jnp.where(position < live_ref[0], value[0, pre : pre + dec], 0.0)
+    copies = [
+        pltpu.make_async_copy(pre_ref, pre_hbm, sems.at[0]),
+        pltpu.make_async_copy(dec_ref, dec_hbm, sems.at[1]),
+    ]
+    for c in copies:
+        c.start()
+    for c in copies:
+        c.wait()
 
 
 def fast_body(n_dp, n_vocab, pre_hidden, dec_hidden, lm_head, pre_targets, dec_targets, dec_live):
@@ -302,7 +321,7 @@
         + [shape((8, BASE), jnp.int32)],
         *map(far, (pre_hidden, dec_hidden, pre_targets)),
         specs=[HBM] * 3,
-        scratch=[pltpu.SMEM(pre_targets.shape, jnp.int32), pltpu.SemaphoreType.DMA((3,))],
+        scratch=[pltpu.SMEM(pre_targets.shape, jnp.int32), pltpu.SemaphoreType.DMA((6,))],
     )
     ids = call(
         functools.partial(digits_kernel, pre), shape((8, BASE), BF16), ids, dec_targets, specs=[VMEM, SMEM]
@@ -334,15 +353,25 @@
     origins = [(0, 0)] + [(ROWS_CROSS, k) for k in (1, 2, 3)] + [(1, 0)] + [(1 - ROWS_CROSS, k) for k in (1, 2, 3)]
     group = n_vocab * (pre + dec)
     rows = n_dp * group
-    own, *parts, tgt = call(
-        functools.partial(matmul_kernel, n_dp, pre, voc, origins),
-        [shape((group, voc), F32)] + [shape((group, wide), WIRE)] * (n_dp - 1) + [shape((group, BASE), F32)],
+    late = 1
+    placed = [shape((rows, quarter), F32), shape((group, BASE), F32)]
+    placed_rows = call(
+        functools.partial(early_kernel, n_vocab, pre, origins[:-late]),
+        placed,
+        *bufs[:-late],
+        specs=[VMEM] * (len(bufs) - late),
+    )
+    own, *parts, _, tgt = call(
+        functools.partial(matmul_kernel, n_dp, n_vocab, pre, voc, origins[-late:]),
+        [shape((group, voc), F32)] + [shape((group, wide), WIRE)] * (n_dp - 1) + placed,
         head,
-        *bufs,
-        specs=[VMEM] * (1 + n_vocab),
-        scratch=[pltpu.VMEM((rows, quarter), F32), pltpu.VMEM((rows - group, wide // TILES), F32)],
+        *bufs[-late:],
+        *placed_rows,
+        specs=[VMEM] * (3 + late),
+        scratch=[pltpu.VMEM((rows - group, wide // TILES), F32)],
         limit=16 << 20,
         flops=2 * rows * quarter * voc,
+        aliases={1 + late: n_dp, 2 + late: n_dp + 1},
     )
     parts = [swap(p, f) for p, f in zip(parts, (near_a, near_b, diagonal))]
     stats = call(
@@ -364,6 +393,8 @@
             *others,
             dec_live,
             specs=[VMEM] * 4 + [SMEM],
+            out_specs=[HBM] * 2,
+            scratch=[pltpu.VMEM((pre,), F32), pltpu.VMEM((dec,), F32), pltpu.SemaphoreType.DMA((2,))],
         )
     )
 

time: 47.1 us -> 47.2 us (level)
    pallas_call x9 -> x10, Pallas kernels: 8 us -> 7.93 us  [call(): pl.pallas_call(kernel, out_shape=outs, in_specs=specs, out_specs=out_spec...]
where the time goes in v3:
time: 47.2 us; the launch traced here: 46.9 us
  starting transfers between devices  19.1 us (40%)
  waiting for transfers between devices  17.8 us (38%)
  Pallas kernels  7.93 us (17%)
  between operations  2.04 us (4%)
    ppermute x17, starting transfers between devices, swap(): return lax.ppermute(x, ('dp', 'vocab'), pairs)  19.1 us
    ppermute x17, waiting for transfers between devices, swap(): return lax.ppermute(x, ('dp', 'vocab'), pairs)  17.8 us
    pallas_call x10, Pallas kernels, call(): pl.pallas_call(kernel, out_shape=outs, in_specs=specs, out_specs=out_spec...  7.93 us
  transfers between devices with their start and end apart: 17, of which 9 were waited for; matrix products, arithmetic and copies ran while one was open for 0% of the time, Pallas kernels for 7%

profile of v3, /device:TPU:0, one launch (start us, length us, event | category | flops | bytes accessed | tf_op | source)
XLA Modules:
  0.0 46.9 jit_solution(13955048054926406877)
XLA Ops:
  0.6 0.9 %shard_map.78 = (bf16[4,7168]{1,0:T(4,128)(2,1)S(1)}, bf16[1,7168]{1,0:T(2,128)(2,1)S(1)}, bf16[8,1152]{1,0:T(8,128)(2,1)S(1)}, bf16[8,1152]{1,0:T(8,128)(2,1)S(1)}, s32[8,128]{1,0:T(8,128)S(1)}) custom-call(bf16[4,7168]{1,0:T(4,128)(2,1)} %pre_hbm.1, bf16[1,7168]{1,0:T(2,128)(2,1)} %dec_hbm.1, s32[4]{0:T(128)} %pt_hbm.1), custom_call_target="tpu_custom_call" | custom-call | tf_op jit(solution)/shard_map/pallas_call | solution.py:25
  1.5 0.6 %collective-permute-start = (bf16[8,1152]{1,0:T(8,128)(2,1)S(1)}, bf16[8,1152]{1,0:T(8,128)(2,1)S(1)}, u32[]{:S(2)}, u32[]{:S(2)}) collective-permute-start(bf16[8,1152]{1,0:T(8,128)(2,1)S(1)} %get-tuple-element.16), channel_id=1, source_target_pairs={{0,1},{1,0},{2,3},{3,2},{4,5},{5,4},{6,7},{7,6},{8,9},{9,8},{10,11... | collective-permute-start | bytes 55304 | tf_op jit(solution)/shard_map/ppermute | solution.py:292
  2.1 0.8 %collective-permute-done.cross_ref = bf16[8,1152]{1,0:T(8,128)(2,1)S(1)} collective-permute-done((bf16[8,1152]{1,0:T(8,128)(2,1)S(1)}, bf16[8,1152]{1,0:T(8,128)(2,1)S(1)}, u32[]{:S(2)}, u32[]{:S(2)}) %collective-permute-start) | collective-permute-done | bytes 18464 | tf_op jit(solution)/shard_map/ppermute | solution.py:292
  3.0 2.6 %collective-permute-start.1 = (bf16[8,2304]{1,0:T(8,128)(2,1)S(1)}, bf16[8,2304]{1,0:T(8,128)(2,1)S(1)}, u32[]{:S(2)}, u32[]{:S(2)}) collective-permute-start(bf16[8,2304]{1,0:T(8,128)(2,1)S(1)} %shard_map.79), channel_id=1, source_target_pairs={{0,9},{1,16},{2,11},{3,18},{4,13},{5,20},{6,15},{7,22},{8,1},{9,24... | collective-permute-start | bytes 110600 | tf_op jit(solution)/shard_map/ppermute | solution.py:292
  5.6 1.4 %collective-permute-start.2 = (bf16[8,1152]{1,0:T(8,128)(2,1)S(1)}, bf16[8,1152]{1,0:T(8,128)(2,1)S(1)}, u32[]{:S(2)}, u32[]{:S(2)}) collective-permute-start(bf16[8,1152]{1,0:T(8,128)(2,1)S(1)} %get-tuple-element.17), channel_id=1, source_target_pairs={{0,25},{1,24},{2,27},{3,26},{4,29},{5,28},{6,31},{7,30},{8,17},{9,... | collective-permute-start | bytes 55304 | tf_op jit(solution)/shard_map/ppermute | solution.py:292
  7.7 2.0 %collective-permute-done.2.diag_ref = bf16[8,1152]{1,0:T(8,128)(2,1)S(1)} collective-permute-done((bf16[8,1152]{1,0:T(8,128)(2,1)S(1)}, bf16[8,1152]{1,0:T(8,128)(2,1)S(1)}, u32[]{:S(2)}, u32[]{:S(2)}) %collective-permute-start.2) | collective-permute-done | bytes 18464 | tf_op jit(solution)/shard_map/ppermute | solution.py:292
  9.7 0.0 collective-permute-done.1.near_ref
  9.8 1.6 %collective-permute-start.5 = (bf16[8,4608]{1,0:T(8,128)(2,1)S(1)}, bf16[8,4608]{1,0:T(8,128)(2,1)S(1)}, u32[]{:S(2)}, u32[]{:S(2)}) collective-permute-start(bf16[8,4608]{1,0:T(8,128)(2,1)S(1)} %shard_map.81.refs_0_), channel_id=1, source_target_pairs={{0,3},{1,2},{2,1},{3,0},{4,7},{5,6},{6,5},{7,4},{8,11},{9,10},{10,... | collective-permute-start | bytes 221192 | tf_op jit(solution)/shard_map/ppermute | solution.py:292
  11.4 2.3 %collective-permute-start.6 = (bf16[8,4608]{1,0:T(8,128)(2,1)S(1)}, bf16[8,4608]{1,0:T(8,128)(2,1)S(1)}, u32[]{:S(2)}, u32[]{:S(2)}) collective-permute-start(bf16[8,4608]{1,0:T(8,128)(2,1)S(1)} %shard_map.81.refs_0_), channel_id=1, source_target_pairs={{0,5},{1,4},{2,7},{3,6},{4,1},{5,0},{6,3},{7,2},{8,13},{9,12},{10,... | collective-permute-start | bytes 221192 | tf_op jit(solution)/shard_map/ppermute | solution.py:292
  13.7 0.2 collective-permute-start.3
  13.9 0.2 collective-permute-start.7
  14.1 0.0 collective-permute-done.5.refs_1_
  14.1 0.3 collective-permute-start.8
  14.4 3.7 %collective-permute-done.6.refs_2_ = bf16[8,4608]{1,0:T(8,128)(2,1)S(1)} collective-permute-done((bf16[8,4608]{1,0:T(8,128)(2,1)S(1)}, bf16[8,4608]{1,0:T(8,128)(2,1)S(1)}, u32[]{:S(2)}, u32[]{:S(2)}) %collective-permute-start.6) | collective-permute-done | bytes 73760 | tf_op jit(solution)/shard_map/ppermute | solution.py:292
  18.1 2.0 %collective-permute-start.9 = (bf16[8,4608]{1,0:T(8,128)(2,1)S(1)}, bf16[8,4608]{1,0:T(8,128)(2,1)S(1)}, u32[]{:S(2)}, u32[]{:S(2)}) collective-permute-start(bf16[8,4608]{1,0:T(8,128)(2,1)S(1)} %collective-permute-done.6.refs_2_), channel_id=1, source_target_pairs={{0,1},{1,0},{2,3},{3,2},{4,5},{5,4},{6,7},{7,6},{8,9},{9,8},{10,11... | collective-permute-start | bytes 221192 | tf_op jit(solution)/shard_map/ppermute | solution.py:292
  20.1 0.0 collective-permute-done.3.refs_3_
  20.1 0.0 collective-permute-start.4
  20.1 3.1 %shard_map.77.head_ref = bf16[2020,1792]{1,0:T(8,128)(2,1)S(1)} custom-call(bf16[2020,1792]{1,0:T(8,128)(2,1)} %bitcast.1), custom_call_target="tpu_custom_call" | custom-call | bytes 14479360 | tf_op jit(solution)/shard_map/pallas_call | solution.py:25
  23.3 0.0 collective-permute-done.7.refs_4_
  23.3 0.0 collective-permute-done.8.refs_5_
  23.3 0.0 collective-permute-done.9.refs_6_
  23.3 0.1 shard_map.82
  23.5 0.0 collective-permute-done.4.refs_0_
  23.5 2.4 %shard_map.83 = (f32[40,2020]{1,0:T(8,128)S(1)}, s16[40,2048]{1,0:T(8,128)(2,1)S(1)}, s16[40,2048]{1,0:T(8,128)(2,1)S(1)}, s16[40,2048]{1,0:T(8,128)(2,1)S(1)}, ...) custom-call(bf16[2020,1792]{1,0:T(8,128)(2,1)S(1)} %shard_map.77.head_ref, ...), custom_call_target="tpu_custom_call", output_to_operand_aliasing={{4}: (2, {}), {5}: (3, {})} | custom-call | flops 1158348800 | tf_op jit(solution)/shard_map/pallas_call | solution.py:25
  25.9 1.2 %collective-permute-start.10 = (s16[40,2048]{1,0:T(8,128)(2,1)S(1)}, s16[40,2048]{1,0:T(8,128)(2,1)S(1)}, u32[]{:S(2)}, u32[]{:S(2)}) collective-permute-start(s16[40,2048]{1,0:T(8,128)(2,1)S(1)} %get-tuple-element.22), channel_id=1, source_target_pairs={{0,16},{1,9},{2,18},{3,11},{4,20},{5,13},{6,22},{7,15},{8,24},{9,1... | collective-permute-start | bytes 491528 | tf_op jit(solution)/shard_map/ppermute | solution.py:292
  27.1 0.9 %collective-permute-start.11 = (s16[40,2048]{1,0:T(8,128)(2,1)S(1)}, s16[40,2048]{1,0:T(8,128)(2,1)S(1)}, u32[]{:S(2)}, u32[]{:S(2)}) collective-permute-start(s16[40,2048]{1,0:T(8,128)(2,1)S(1)} %get-tuple-element.23), channel_id=1, source_target_pairs={{0,8},{1,17},{2,10},{3,19},{4,12},{5,21},{6,14},{7,23},{8,0},{9,25... | collective-permute-start | bytes 491528 | tf_op jit(solution)/shard_map/ppermute | solution.py:292
  28.0 1.4 %collective-permute-start.12 = (s16[40,2048]{1,0:T(8,128)(2,1)S(1)}, s16[40,2048]{1,0:T(8,128)(2,1)S(1)}, u32[]{:S(2)}, u32[]{:S(2)}) collective-permute-start(s16[40,2048]{1,0:T(8,128)(2,1)S(1)} %get-tuple-element.24), channel_id=1, source_target_pairs={{0,24},{1,25},{2,26},{3,27},{4,28},{5,29},{6,30},{7,31},{8,16},{9,... | collective-permute-start | bytes 491528 | tf_op jit(solution)/shard_map/ppermute | solution.py:292
  29.5 3.5 %collective-permute-done.10.p1 = s16[40,2048]{1,0:T(8,128)(2,1)S(1)} collective-permute-done((s16[40,2048]{1,0:T(8,128)(2,1)S(1)}, s16[40,2048]{1,0:T(8,128)(2,1)S(1)}, u32[]{:S(2)}, u32[]{:S(2)}) %collective-permute-start.10) | collective-permute-done | bytes 163872 | tf_op jit(solution)/shard_map/ppermute | solution.py:292
  33.0 0.8 %collective-permute-done.11.p2 = s16[40,2048]{1,0:T(8,128)(2,1)S(1)} collective-permute-done((s16[40,2048]{1,0:T(8,128)(2,1)S(1)}, s16[40,2048]{1,0:T(8,128)(2,1)S(1)}, u32[]{:S(2)}, u32[]{:S(2)}) %collective-permute-start.11) | collective-permute-done | bytes 163872 | tf_op jit(solution)/shard_map/ppermute | solution.py:292
  33.8 2.9 %collective-permute-done.12.p3 = s16[40,2048]{1,0:T(8,128)(2,1)S(1)} collective-permute-done((s16[40,2048]{1,0:T(8,128)(2,1)S(1)}, s16[40,2048]{1,0:T(8,128)(2,1)S(1)}, u32[]{:S(2)}, u32[]{:S(2)}) %collective-permute-start.12) | collective-permute-done | bytes 163872 | tf_op jit(solution)/shard_map/ppermute | solution.py:292
  36.7 0.4 shard_map.84.mine_ref
  37.1 0.0 collective-permute-start.13
  37.1 1.2 %collective-permute-done.13.other_ref = f32[8,128]{1,0:T(8,128)S(1)} collective-permute-done((f32[8,128]{1,0:T(8,128)S(1)}, f32[8,128]{1,0:T(8,128)S(1)}, u32[]{:S(2)}, u32[]{:S(2)}) %collective-permute-start.13) | collective-permute-done | bytes 4128 | tf_op jit(solution)/shard_map/ppermute | solution.py:292
  38.3 0.1 shard_map.85.mine_ref
  38.4 1.8 %collective-permute-start.14 = (f32[8,128]{1,0:T(8,128)S(1)}, f32[8,128]{1,0:T(8,128)S(1)}, u32[]{:S(2)}, u32[]{:S(2)}) collective-permute-start(f32[8,128]{1,0:T(8,128)S(1)} %shard_map.85.mine_ref), channel_id=1, source_target_pairs={{0,3},{1,2},{2,1},{3,0},{4,7},{5,6},{6,5},{7,4},{8,11},{9,10},{10,... | collective-permute-start | bytes 12296 | tf_op jit(solution)/shard_map/ppermute | solution.py:292
  40.2 1.2 %collective-permute-start.15 = (f32[8,128]{1,0:T(8,128)S(1)}, f32[8,128]{1,0:T(8,128)S(1)}, u32[]{:S(2)}, u32[]{:S(2)}) collective-permute-start(f32[8,128]{1,0:T(8,128)S(1)} %shard_map.85.mine_ref), channel_id=1, source_target_pairs={{0,5},{1,4},{2,7},{3,6},{4,1},{5,0},{6,3},{7,2},{8,13},{9,12},{10,... | collective-permute-start | bytes 12296 | tf_op jit(solution)/shard_map/ppermute | solution.py:292
  41.3 1.2 %collective-permute-start.16 = (f32[8,128]{1,0:T(8,128)S(1)}, f32[8,128]{1,0:T(8,128)S(1)}, u32[]{:S(2)}, u32[]{:S(2)}) collective-permute-start(f32[8,128]{1,0:T(8,128)S(1)} %shard_map.85.mine_ref), channel_id=1, source_target_pairs={{0,7},{1,6},{2,5},{3,4},{4,3},{5,2},{6,1},{7,0},{8,15},{9,14},{10,... | collective-permute-start | bytes 12296 | tf_op jit(solution)/shard_map/ppermute | solution.py:292
  43.2 0.0 collective-permute-done.14.r1
  43.2 0.9 %collective-permute-done.15.r2 = f32[8,128]{1,0:T(8,128)S(1)} collective-permute-done((f32[8,128]{1,0:T(8,128)S(1)}, f32[8,128]{1,0:T(8,128)S(1)}, u32[]{:S(2)}, u32[]{:S(2)}) %collective-permute-start.15) | collective-permute-done | bytes 4128 | tf_op jit(solution)/shard_map/ppermute | solution.py:292
  44.1 2.1 %collective-permute-done.16.r3 = f32[8,128]{1,0:T(8,128)S(1)} collective-permute-done((f32[8,128]{1,0:T(8,128)S(1)}, f32[8,128]{1,0:T(8,128)S(1)}, u32[]{:S(2)}, u32[]{:S(2)}) %collective-permute-start.16) | collective-permute-done | bytes 4128 | tf_op jit(solution)/shard_map/ppermute | solution.py:292
  46.2 0.7 %shard_map.86 = (f32[4]{0:T(128)}, f32[1]{0:T(128)}) custom-call(f32[8,128]{1,0:T(8,128)S(1)} %shard_map.85.mine_ref, f32[8,128]{1,0:T(8,128)S(1)} %collective-permute-done.14.r1, f32[8,128]{1,0:T(8,128)S(1)} %collective-permute-done.15.r2, f32[8,128]{1,0:T(8,128)S(1)} %collective-permute-done.16.r3, s32[1]{0:T(128)S(6)} %copy.13.live_ref), custom_call_target="tpu_custom_call" | custom-call | tf_op jit(solution)/shard_map/pallas_call | solution.py:25
  (3 shorter events, 0.1 us)
Async XLA Ops:
  1.5 1.4 %collective-permute-start = (bf16[8,1152]{1,0:T(8,128)(2,1)S(1)}, bf16[8,1152]{1,0:T(8,128)(2,1)S(1)}, u32[]{:S(2)}, u32[]{:S(2)}) collective-permute-start(bf16[8,1152]{1,0:T(8,128)(2,1)S(1)} %get-tuple-element.16), channel_id=1, source_target_pairs={{0,1},{1,0},{2,3},{3,2},{4,5},{5,4},{6,7},{7,6},{8,9},{9,8},{10,11... | collective-permute-start | bytes 55304 | tf_op jit(solution)/shard_map/ppermute | solution.py:292
  3.0 6.7 %collective-permute-start.1 = (bf16[8,2304]{1,0:T(8,128)(2,1)S(1)}, bf16[8,2304]{1,0:T(8,128)(2,1)S(1)}, u32[]{:S(2)}, u32[]{:S(2)}) collective-permute-start(bf16[8,2304]{1,0:T(8,128)(2,1)S(1)} %shard_map.79), channel_id=1, source_target_pairs={{0,9},{1,16},{2,11},{3,18},{4,13},{5,20},{6,15},{7,22},{8,1},{9,24... | collective-permute-start | bytes 110600 | tf_op jit(solution)/shard_map/ppermute | solution.py:292
  5.6 4.1 %collective-permute-start.2 = (bf16[8,1152]{1,0:T(8,128)(2,1)S(1)}, bf16[8,1152]{1,0:T(8,128)(2,1)S(1)}, u32[]{:S(2)}, u32[]{:S(2)}) collective-permute-start(bf16[8,1152]{1,0:T(8,128)(2,1)S(1)} %get-tuple-element.17), channel_id=1, source_target_pairs={{0,25},{1,24},{2,27},{3,26},{4,29},{5,28},{6,31},{7,30},{8,17},{9,... | collective-permute-start | bytes 55304 | tf_op jit(solution)/shard_map/ppermute | solution.py:292
  9.8 4.3 %collective-permute-start.5 = (bf16[8,4608]{1,0:T(8,128)(2,1)S(1)}, bf16[8,4608]{1,0:T(8,128)(2,1)S(1)}, u32[]{:S(2)}, u32[]{:S(2)}) collective-permute-start(bf16[8,4608]{1,0:T(8,128)(2,1)S(1)} %shard_map.81.refs_0_), channel_id=1, source_target_pairs={{0,3},{1,2},{2,1},{3,0},{4,7},{5,6},{6,5},{7,4},{8,11},{9,10},{10,... | collective-permute-start | bytes 221192 | tf_op jit(solution)/shard_map/ppermute | solution.py:292
  11.4 6.7 %collective-permute-start.6 = (bf16[8,4608]{1,0:T(8,128)(2,1)S(1)}, bf16[8,4608]{1,0:T(8,128)(2,1)S(1)}, u32[]{:S(2)}, u32[]{:S(2)}) collective-permute-start(bf16[8,4608]{1,0:T(8,128)(2,1)S(1)} %shard_map.81.refs_0_), channel_id=1, source_target_pairs={{0,5},{1,4},{2,7},{3,6},{4,1},{5,0},{6,3},{7,2},{8,13},{9,12},{10,... | collective-permute-start | bytes 221192 | tf_op jit(solution)/shard_map/ppermute | solution.py:292
  13.7 6.4 %collective-permute-start.3 = (bf16[8,4608]{1,0:T(8,128)(2,1)S(1)}, bf16[8,4608]{1,0:T(8,128)(2,1)S(1)}, u32[]{:S(2)}, u32[]{:S(2)}) collective-permute-start(bf16[8,4608]{1,0:T(8,128)(2,1)S(1)} %shard_map.81.refs_0_), channel_id=1, source_target_pairs={{0,7},{1,6},{2,5},{3,4},{4,3},{5,2},{6,1},{7,0},{8,15},{9,14},{10,... | collective-permute-start | bytes 221192 | tf_op jit(solution)/shard_map/ppermute | solution.py:292
  13.9 9.4 %collective-permute-start.7 = (bf16[8,4608]{1,0:T(8,128)(2,1)S(1)}, bf16[8,4608]{1,0:T(8,128)(2,1)S(1)}, u32[]{:S(2)}, u32[]{:S(2)}) collective-permute-start(bf16[8,4608]{1,0:T(8,128)(2,1)S(1)} %shard_map.81.refs_0_), channel_id=1, source_target_pairs={{0,1},{1,0},{2,3},{3,2},{4,5},{5,4},{6,7},{7,6},{8,9},{9,8},{10,11... | collective-permute-start | bytes 221192 | tf_op jit(solution)/shard_map/ppermute | solution.py:292
  14.1 9.2 %collective-permute-start.8 = (bf16[8,4608]{1,0:T(8,128)(2,1)S(1)}, bf16[8,4608]{1,0:T(8,128)(2,1)S(1)}, u32[]{:S(2)}, u32[]{:S(2)}) collective-permute-start(bf16[8,4608]{1,0:T(8,128)(2,1)S(1)} %collective-permute-done.5.refs_1_), channel_id=1, source_target_pairs={{0,1},{1,0},{2,3},{3,2},{4,5},{5,4},{6,7},{7,6},{8,9},{9,8},{10,11... | collective-permute-start | bytes 221192 | tf_op jit(solution)/shard_map/ppermute | solution.py:292
  18.1 5.2 %collective-permute-start.9 = (bf16[8,4608]{1,0:T(8,128)(2,1)S(1)}, bf16[8,4608]{1,0:T(8,128)(2,1)S(1)}, u32[]{:S(2)}, u32[]{:S(2)}) collective-permute-start(bf16[8,4608]{1,0:T(8,128)(2,1)S(1)} %collective-permute-done.6.refs_2_), channel_id=1, source_target_pairs={{0,1},{1,0},{2,3},{3,2},{4,5},{5,4},{6,7},{7,6},{8,9},{9,8},{10,11... | collective-permute-start | bytes 221192 | tf_op jit(solution)/shard_map/ppermute | solution.py:292
  20.1 3.3 %collective-permute-start.4 = (bf16[8,4608]{1,0:T(8,128)(2,1)S(1)}, bf16[8,4608]{1,0:T(8,128)(2,1)S(1)}, u32[]{:S(2)}, u32[]{:S(2)}) collective-permute-start(bf16[8,4608]{1,0:T(8,128)(2,1)S(1)} %collective-permute-done.3.refs_3_), channel_id=1, source_target_pairs={{0,1},{1,0},{2,3},{3,2},{4,5},{5,4},{6,7},{7,6},{8,9},{9,8},{10,11... | collective-permute-start | bytes 221192 | tf_op jit(solution)/shard_map/ppermute | solution.py:292
  25.9 7.1 %collective-permute-start.10 = (s16[40,2048]{1,0:T(8,128)(2,1)S(1)}, s16[40,2048]{1,0:T(8,128)(2,1)S(1)}, u32[]{:S(2)}, u32[]{:S(2)}) collective-permute-start(s16[40,2048]{1,0:T(8,128)(2,1)S(1)} %get-tuple-element.22), channel_id=1, source_target_pairs={{0,16},{1,9},{2,18},{3,11},{4,20},{5,13},{6,22},{7,15},{8,24},{9,1... | collective-permute-start | bytes 491528 | tf_op jit(solution)/shard_map/ppermute | solution.py:292
  27.1 6.7 %collective-permute-start.11 = (s16[40,2048]{1,0:T(8,128)(2,1)S(1)}, s16[40,2048]{1,0:T(8,128)(2,1)S(1)}, u32[]{:S(2)}, u32[]{:S(2)}) collective-permute-start(s16[40,2048]{1,0:T(8,128)(2,1)S(1)} %get-tuple-element.23), channel_id=1, source_target_pairs={{0,8},{1,17},{2,10},{3,19},{4,12},{5,21},{6,14},{7,23},{8,0},{9,25... | collective-permute-start | bytes 491528 | tf_op jit(solution)/shard_map/ppermute | solution.py:292
  28.0 8.6 %collective-permute-start.12 = (s16[40,2048]{1,0:T(8,128)(2,1)S(1)}, s16[40,2048]{1,0:T(8,128)(2,1)S(1)}, u32[]{:S(2)}, u32[]{:S(2)}) collective-permute-start(s16[40,2048]{1,0:T(8,128)(2,1)S(1)} %get-tuple-element.24), channel_id=1, source_target_pairs={{0,24},{1,25},{2,26},{3,27},{4,28},{5,29},{6,30},{7,31},{8,16},{9,... | collective-permute-start | bytes 491528 | tf_op jit(solution)/shard_map/ppermute | solution.py:292
  37.1 1.2 %collective-permute-start.13 = (f32[8,128]{1,0:T(8,128)S(1)}, f32[8,128]{1,0:T(8,128)S(1)}, u32[]{:S(2)}, u32[]{:S(2)}) collective-permute-start(f32[8,128]{1,0:T(8,128)S(1)} %shard_map.84.mine_ref), channel_id=1, source_target_pairs={{0,1},{1,0},{2,3},{3,2},{4,5},{5,4},{6,7},{7,6},{8,9},{9,8},{10,11... | collective-permute-start | bytes 12296 | tf_op jit(solution)/shard_map/ppermute | solution.py:292
  38.4 4.8 %collective-permute-start.14 = (f32[8,128]{1,0:T(8,128)S(1)}, f32[8,128]{1,0:T(8,128)S(1)}, u32[]{:S(2)}, u32[]{:S(2)}) collective-permute-start(f32[8,128]{1,0:T(8,128)S(1)} %shard_map.85.mine_ref), channel_id=1, source_target_pairs={{0,3},{1,2},{2,1},{3,0},{4,7},{5,6},{6,5},{7,4},{8,11},{9,10},{10,... | collective-permute-start | bytes 12296 | tf_op jit(solution)/shard_map/ppermute | solution.py:292
  40.2 3.9 %collective-permute-start.15 = (f32[8,128]{1,0:T(8,128)S(1)}, f32[8,128]{1,0:T(8,128)S(1)}, u32[]{:S(2)}, u32[]{:S(2)}) collective-permute-start(f32[8,128]{1,0:T(8,128)S(1)} %shard_map.85.mine_ref), channel_id=1, source_target_pairs={{0,5},{1,4},{2,7},{3,6},{4,1},{5,0},{6,3},{7,2},{8,13},{9,12},{10,... | collective-permute-start | bytes 12296 | tf_op jit(solution)/shard_map/ppermute | solution.py:292
  41.3 4.8 %collective-permute-start.16 = (f32[8,128]{1,0:T(8,128)S(1)}, f32[8,128]{1,0:T(8,128)S(1)}, u32[]{:S(2)}, u32[]{:S(2)}) collective-permute-start(f32[8,128]{1,0:T(8,128)S(1)} %shard_map.85.mine_ref), channel_id=1, source_target_pairs={{0,7},{1,6},{2,5},{3,4},{4,3},{5,2},{6,1},{7,0},{8,15},{9,14},{10,... | collective-permute-start | bytes 12296 | tf_op jit(solution)/shard_map/ppermute | solution.py:292
